TPU v7x, 256 devices: a whole 4x4x8 slice. The times are simulated.
256 devices in a mesh: section: 16 (over z_hi, y, core), seq: 16 (over x, z_lo).
Axes of the slice: x: 4, y: 4, z: 8 (z_hi: 2, z_lo: 4; z = z_hi * 4 + z_lo), core: 2. Of those that a mesh axis runs over, the one named last changes fastest.
Arguments:
- base_ids: int32 [2, 2048], P(None, 'seq'), may hold values from 0 to 3
- stem_weight: bfloat16 [15, 4, 768], replicated, may hold values from -1.5 to 1.5
- conv_weight: bfloat16 [16, 5, 768, 768], P('section'), may hold values from -0.09375 to 0.09375
- block_gain: float32 [16, 768], P('section'), may hold values from 0.1 to 1.9
- cotangent: bfloat16 [2, 2048, 768], P(None, 'seq'), may hold values from -0.29882812 to 0.29882812
Outputs:
- conv_grad: bfloat16 [16, 5, 768, 768], P('section', None, 'seq')
- gain_grad: float32 [16, 768], P('section', 'seq')
All inputs are finite; a program needn't handle non-finite values.
Results may differ from a plain program's by a relative error of at most 0.035.
Values may be sent and summed in bfloat16 or wider, within the bound.
No kernel may reach another device: no remote copies, remote signals or barrier semaphores. Data moves between devices by JAX's collectives and lax.ppermute only.
A program may use at most 128 MiB of HBM per device.

v0:
```python
import jax
import jax.numpy as jnp
from jax import lax
from jax.sharding import PartitionSpec as P

KERNEL = 5
STEM_K = 15
BASES = 4


def padded_2(array, sides, width):
    for axis, dim in sides:
        size, length = (lax.axis_size(axis), array.shape[dim])
        up = [(i, (i + 1) % size) for i in range(size - 1)]
        down = [(j, i) for i, j in up]
        last = lax.slice_in_dim(array, length - width, length, axis=dim)
        initial = lax.slice_in_dim(array, 0, width, axis=dim)
        before = lax.ppermute(last, axis, up)
        after = lax.ppermute(initial, axis, down)
        array = jnp.concatenate([before, array, after], axis=dim)
    return array


def passed_along(block, axis, distance):
    devices = range(lax.axis_size(axis))
    route = [(i - distance, i) for i in devices if i - distance in devices]
    return lax.ppermute(block, axis, route)


def activate(block_sum, gain_row):
    scale = lax.rsqrt(jnp.mean(block_sum * block_sum, axis=-1, keepdims=True) + 1e-06)
    return jax.nn.gelu(block_sum * scale * gain_row)


def mirror(payload):
    section_count = lax.axis_size("section")
    spread = lax.all_to_all(payload, "section", split_axis=0, concat_axis=0, tiled=True)
    flipped = spread.reshape(section_count, -1, payload.shape[1])[::-1].reshape(payload.shape)
    moved = lax.all_to_all(flipped, "section", split_axis=0, concat_axis=0, tiled=True)
    return moved


def put_slot(buffer, value, slot_index, accepted):
    previous = lax.dynamic_index_in_dim(buffer, slot_index, 0, keepdims=False)
    return lax.dynamic_update_index_in_dim(
        buffer, jnp.where(accepted, value, previous), slot_index, 0
    )


def shards(base_ids, stem_weight, conv_weight, block_gain, cotangent):
    section_count = lax.axis_size("section")
    my_section = lax.axis_index("section")
    half_count = section_count // 2
    micro_count, row_count, channels = cotangent.shape
    conv_reach = (KERNEL - 1) // 2
    stem_reach = (STEM_K - 1) // 2
    filters = conv_weight[0]
    gain_row = block_gain[0]
    is_first = my_section == 0
    is_last = my_section == section_count - 1
    decoder = my_section >= half_count
    encoder = my_section < half_count
    padded_ids = padded_2(base_ids + 1, (("seq", 1),), stem_reach)
    letters = jnp.arange(1, BASES + 1, dtype=jnp.int32)
    matches = [
        padded_ids[:, offset : offset + row_count, None] == letters for offset in range(STEM_K)
    ]
    onehot = jnp.concatenate(matches, axis=2).astype(jnp.bfloat16)
    stem_out = jnp.einsum(
        "ohs,sn->ohn",
        onehot,
        stem_weight.reshape(STEM_K * BASES, channels),
        preferred_element_type=jnp.float32,
    ).astype(jnp.bfloat16)
    empty_tile = jnp.zeros((row_count, channels), jnp.bfloat16)

    def conv_out(block_sum, padded):
        summed = block_sum
        for offset in range(KERNEL):
            summed = summed + jnp.dot(
                padded[offset : offset + row_count],
                filters[offset],
                preferred_element_type=jnp.float32,
            )
        return summed.astype(jnp.bfloat16)

    def forward_tick(tick, state_tuple, sending):
        inflow, skip_store, stored_sums, stored_rows = state_tuple
        micro_slot = tick - my_section
        active = (micro_slot >= 0) & (micro_slot < micro_count)
        slot_index = jnp.clip(micro_slot, 0, micro_count - 1)
        from_stem = lax.dynamic_index_in_dim(stem_out, slot_index, 0, keepdims=False)
        block_in = jnp.where(is_first, from_stem, inflow)
        joined = lax.dynamic_index_in_dim(skip_store, slot_index, 0, keepdims=False)
        block_sum = block_in.astype(jnp.float32) + jnp.where(
            decoder, joined.astype(jnp.float32), 0.0
        )
        activated = activate(block_sum, gain_row).astype(jnp.bfloat16)
        padded = padded_2(activated, (("seq", 0),), conv_reach)
        block_out = lax.cond(
            active & jnp.logical_not(is_last),
            lambda: conv_out(block_sum, padded),
            lambda: empty_tile,
        )
        stored_sums = put_slot(stored_sums, block_sum, slot_index, active)
        stored_rows = put_slot(stored_rows, padded, slot_index, active)
        if sending:
            arrived = mirror(block_out)
            mirror_slot = tick - (section_count - 1 - my_section)
            accepted = decoder & (mirror_slot >= 0) & (mirror_slot < micro_count)
            mirror_index = jnp.clip(mirror_slot, 0, micro_count - 1)
            skip_store = put_slot(skip_store, arrived, mirror_index, accepted)
        inflow = passed_along(block_out, "section", 1)
        return (inflow, skip_store, stored_sums, stored_rows)

    rows_start = jnp.zeros((micro_count, row_count + 2 * conv_reach, channels), jnp.bfloat16)
    split_tick = half_count + micro_count - 1
    tick_count = section_count + micro_count - 1
    state_tuple = (
        empty_tile,
        jnp.zeros((micro_count, row_count, channels), jnp.bfloat16),
        jnp.zeros((micro_count, row_count, channels), jnp.float32),
        rows_start,
    )
    state_tuple = lax.fori_loop(
        0, split_tick, lambda tick, held: forward_tick(tick, held, True), state_tuple
    )
    state_tuple = lax.fori_loop(
        split_tick, tick_count, lambda tick, held: forward_tick(tick, held, False), state_tuple
    )
    unused_flow, unused_skips, stored_sums, stored_rows = state_tuple

    def backward_tick(tick, state_tuple, sending):
        grad_flow, skip_grads, kernel_sum, gain_sum = state_tuple
        micro_slot = tick - (section_count - 1 - my_section)
        active = (micro_slot >= 0) & (micro_slot < micro_count)
        slot_index = jnp.clip(micro_slot, 0, micro_count - 1)
        from_cot = lax.dynamic_index_in_dim(cotangent, slot_index, 0, keepdims=False)
        from_next = jnp.where(is_last, from_cot, grad_flow).astype(jnp.float32)
        from_skip = lax.dynamic_index_in_dim(skip_grads, slot_index, 0, keepdims=False)
        grad_out = (from_next + jnp.where(encoder, from_skip.astype(jnp.float32), 0.0)).astype(
            jnp.bfloat16
        )
        block_sum = lax.dynamic_index_in_dim(stored_sums, slot_index, 0, keepdims=False)
        padded = lax.dynamic_index_in_dim(stored_rows, slot_index, 0, keepdims=False)
        grad_padded = padded_2(grad_out, (("seq", 0),), conv_reach)

        def backward_block():
            kernel_terms = jnp.stack(
                [
                    jnp.einsum(
                        "rc,rd->cd",
                        padded[offset : offset + row_count],
                        grad_out,
                        preferred_element_type=jnp.float32,
                    )
                    for offset in range(KERNEL)
                ]
            )
            grad_act = jnp.zeros((row_count, channels), jnp.float32)
            for offset in range(KERNEL):
                start = 2 * conv_reach - offset
                grad_act = grad_act + jnp.einsum(
                    "rd,cd->rc",
                    grad_padded[start : start + row_count],
                    filters[offset],
                    preferred_element_type=jnp.float32,
                )
            unused_out, pullback = jax.vjp(activate, block_sum, gain_row)
            grad_norm_in, grad_gain = pullback(grad_act)
            grad_in = (grad_out.astype(jnp.float32) + grad_norm_in).astype(jnp.bfloat16)
            return (kernel_sum + kernel_terms, gain_sum + grad_gain, grad_in)

        def unused_block():
            return (kernel_sum, gain_sum, empty_tile)

        kernel_sum, gain_sum, grad_in = lax.cond(active, backward_block, unused_block)
        if sending:
            arrived = mirror(grad_in)
            return_slot = tick - my_section
            accepted = encoder & (return_slot >= 0) & (return_slot < micro_count)
            return_index = jnp.clip(return_slot, 0, micro_count - 1)
            skip_grads = put_slot(skip_grads, arrived, return_index, accepted)
        grad_flow = passed_along(grad_in, "section", -1)
        return (grad_flow, skip_grads, kernel_sum, gain_sum)

    state_tuple = (
        empty_tile,
        jnp.zeros((micro_count, row_count, channels), jnp.bfloat16),
        jnp.zeros((KERNEL, channels, channels), jnp.float32),
        jnp.zeros((channels,), jnp.float32),
    )
    state_tuple = lax.fori_loop(
        0, split_tick, lambda tick, held: backward_tick(tick, held, True), state_tuple
    )
    state_tuple = lax.fori_loop(
        split_tick, tick_count, lambda tick, held: backward_tick(tick, held, False), state_tuple
    )
    unused_flow, unused_grads, kernel_sum, gain_sum = state_tuple
    kernel_part, gain_part = (
        lax.psum_scatter(
            kernel_sum.astype(jnp.bfloat16), "seq", scatter_dimension=1, tiled=True
        ).astype(jnp.float32),
        lax.psum_scatter(
            gain_sum.astype(jnp.bfloat16), "seq", scatter_dimension=0, tiled=True
        ).astype(jnp.float32),
    )
    return (kernel_part.astype(jnp.bfloat16)[None], gain_part[None])


def solution(mesh):
    placed = (
        P(None, "seq"),
        P(),
        P("section", None, None, None),
        P("section", None),
        P(None, "seq", None),
    )
    return jax.shard_map(
        shards,
        mesh=mesh,
        in_specs=placed,
        out_specs=(P("section", None, "seq", None), P("section", "seq")),
        check_vma=False,
    )
```

profile of v0, /device:TPU:1, one launch (start us, length us, event | category | flops | bytes accessed | tf_op | source)
XLA Modules:
  0.0 1792.4 jit_solution(477611050527207096)
XLA Ops:
  16.2 439.5 %while.79 = (s32[]{:T(128)}, bf16[128,768]{1,0:T(8,128)(2,1)S(1)}, bf16[2,128,768]{2,1,0:T(8,128)(2,1)S(1)}, f32[2,128,768]{2,1,0:T(8,128)S(1)}, bf16[2,132,768]...) while((s32[]{:T(128)}, bf16[128,768]{1,0:T(8,128)(2,1)S(1)}, ...), condition=%wide.region_4.5_spmd, body=%wide.region_0.4_spmd.sunk | while | flops 759929984 | bytes 18576368 | solution.py:125
  23.8 25.4 %all_to_all.66 = bf16[16,8,768]{2,1,0:T(8,128)(2,1)S(1)} all-to-all(bf16[16,8,768]{2,1,0:T(8,128)(2,1)S(1)} %bitcast.278), channel_id=1, replica_groups=mesh['section'=16,'seq'=16] {'section'}, dimensions={0} | all-to-all | bytes 393216 | tf_op jit(solution)/shard_map/while/body/eval_jaxpr/all_to_all | solution.py:37
  80.7 14.8 all_to_all.66
  127.5 15.1 all_to_all.66
  166.0 21.0 %all_to_all.66 = bf16[16,8,768]{2,1,0:T(8,128)(2,1)S(1)} all-to-all(bf16[16,8,768]{2,1,0:T(8,128)(2,1)S(1)} %bitcast.278), channel_id=1, replica_groups=mesh['section'=16,'seq'=16] {'section'}, dimensions={0} | all-to-all | bytes 393216 | tf_op jit(solution)/shard_map/while/body/eval_jaxpr/all_to_all | solution.py:37
  213.8 21.8 %all_to_all.66 = bf16[16,8,768]{2,1,0:T(8,128)(2,1)S(1)} all-to-all(bf16[16,8,768]{2,1,0:T(8,128)(2,1)S(1)} %bitcast.278), channel_id=1, replica_groups=mesh['section'=16,'seq'=16] {'section'}, dimensions={0} | all-to-all | bytes 393216 | tf_op jit(solution)/shard_map/while/body/eval_jaxpr/all_to_all | solution.py:37
  261.8 21.8 %all_to_all.66 = bf16[16,8,768]{2,1,0:T(8,128)(2,1)S(1)} all-to-all(bf16[16,8,768]{2,1,0:T(8,128)(2,1)S(1)} %bitcast.278), channel_id=1, replica_groups=mesh['section'=16,'seq'=16] {'section'}, dimensions={0} | all-to-all | bytes 393216 | tf_op jit(solution)/shard_map/while/body/eval_jaxpr/all_to_all | solution.py:37
  301.6 9.5 collective-permute-start.1
  312.0 22.3 %all_to_all.66 = bf16[16,8,768]{2,1,0:T(8,128)(2,1)S(1)} all-to-all(bf16[16,8,768]{2,1,0:T(8,128)(2,1)S(1)} %bitcast.278), channel_id=1, replica_groups=mesh['section'=16,'seq'=16] {'section'}, dimensions={0} | all-to-all | bytes 393216 | tf_op jit(solution)/shard_map/while/body/eval_jaxpr/all_to_all | solution.py:37
  352.3 8.5 collective-permute-start.1
  361.6 22.3 %all_to_all.66 = bf16[16,8,768]{2,1,0:T(8,128)(2,1)S(1)} all-to-all(bf16[16,8,768]{2,1,0:T(8,128)(2,1)S(1)} %bitcast.278), channel_id=1, replica_groups=mesh['section'=16,'seq'=16] {'section'}, dimensions={0} | all-to-all | bytes 393216 | tf_op jit(solution)/shard_map/while/body/eval_jaxpr/all_to_all | solution.py:37
  411.2 29.0 %all_to_all.66 = bf16[16,8,768]{2,1,0:T(8,128)(2,1)S(1)} all-to-all(bf16[16,8,768]{2,1,0:T(8,128)(2,1)S(1)} %bitcast.278), channel_id=1, replica_groups=mesh['section'=16,'seq'=16] {'section'}, dimensions={0} | all-to-all | bytes 393216 | tf_op jit(solution)/shard_map/while/body/eval_jaxpr/all_to_all | solution.py:37
  455.7 155.2 %while.80 = (s32[]{:T(128)}, bf16[128,768]{1,0:T(8,128)(2,1)S(1)}, f32[2,128,768]{2,1,0:T(8,128)S(1)}, bf16[2,132,768]{2,1,0:T(8,128)(2,1)S(1)}, s32[]{:T(128)},...) while((s32[]{:T(128)}, bf16[128,768]{1,0:T(8,128)(2,1)S(1)}, ...), condition=%wide.region_9.10_spmd, body=%wide.region_5.9_spmd.sunk | while | flops 759831680 | bytes 16610206 | solution.py:128
  474.9 8.9 collective-permute-start.4
  495.0 8.9 collective-permute-start.4
  597.1 11.2 collective-permute-start.5
  616.4 662.1 %while.81 = (s32[]{:T(128)}, bf16[128,768]{1,0:T(8,128)(2,1)S(1)}, bf16[2,128,768]{2,1,0:T(8,128)(2,1)S(1)}, f32[5,768,768]{2,1,0:T(8,128)}, f32[768]{0:T(1024)S...) while((s32[]{:T(128)}, bf16[128,768]{1,0:T(8,128)(2,1)S(1)}, ...), condition=%wide.region_16.17_spmd, body=%wide.region_10.16_spmd.sunk | while | flops 1518127872 | bytes 83248296 | solution.py:193
  625.8 82.5 %all_to_all.67 = bf16[16,8,768]{2,1,0:T(8,128)(2,1)S(1)} all-to-all(bf16[16,8,768]{2,1,0:T(8,128)(2,1)S(1)} %bitcast.277), channel_id=1, replica_groups=mesh['section'=16,'seq'=16] {'section'}, dimensions={0} | all-to-all | bytes 393216 | tf_op jit(solution)/shard_map/while/body/eval_jaxpr/all_to_all | solution.py:37
  715.3 8.5 all-to-all-done.3
  733.1 43.7 %all_to_all.67 = bf16[16,8,768]{2,1,0:T(8,128)(2,1)S(1)} all-to-all(bf16[16,8,768]{2,1,0:T(8,128)(2,1)S(1)} %bitcast.277), channel_id=1, replica_groups=mesh['section'=16,'seq'=16] {'section'}, dimensions={0} | all-to-all | bytes 393216 | tf_op jit(solution)/shard_map/while/body/eval_jaxpr/all_to_all | solution.py:37
  783.8 8.5 all-to-all-done.3
  801.9 44.2 %all_to_all.67 = bf16[16,8,768]{2,1,0:T(8,128)(2,1)S(1)} all-to-all(bf16[16,8,768]{2,1,0:T(8,128)(2,1)S(1)} %bitcast.277), channel_id=1, replica_groups=mesh['section'=16,'seq'=16] {'section'}, dimensions={0} | all-to-all | bytes 393216 | tf_op jit(solution)/shard_map/while/body/eval_jaxpr/all_to_all | solution.py:37
  853.0 8.5 all-to-all-done.3
  871.1 44.2 %all_to_all.67 = bf16[16,8,768]{2,1,0:T(8,128)(2,1)S(1)} all-to-all(bf16[16,8,768]{2,1,0:T(8,128)(2,1)S(1)} %bitcast.277), channel_id=1, replica_groups=mesh['section'=16,'seq'=16] {'section'}, dimensions={0} | all-to-all | bytes 393216 | tf_op jit(solution)/shard_map/while/body/eval_jaxpr/all_to_all | solution.py:37
  922.2 8.5 all-to-all-done.3
  932.2 8.8 collective-permute-start.7
  941.9 43.7 %all_to_all.67 = bf16[16,8,768]{2,1,0:T(8,128)(2,1)S(1)} all-to-all(bf16[16,8,768]{2,1,0:T(8,128)(2,1)S(1)} %bitcast.277), channel_id=1, replica_groups=mesh['section'=16,'seq'=16] {'section'}, dimensions={0} | all-to-all | bytes 393216 | tf_op jit(solution)/shard_map/while/body/eval_jaxpr/all_to_all | solution.py:37
  992.6 8.5 all-to-all-done.3
  1002.6 8.9 collective-permute-start.7
  1012.3 42.7 %all_to_all.67 = bf16[16,8,768]{2,1,0:T(8,128)(2,1)S(1)} all-to-all(bf16[16,8,768]{2,1,0:T(8,128)(2,1)S(1)} %bitcast.277), channel_id=1, replica_groups=mesh['section'=16,'seq'=16] {'section'}, dimensions={0} | all-to-all | bytes 393216 | tf_op jit(solution)/shard_map/while/body/eval_jaxpr/all_to_all | solution.py:37
  1061.9 8.5 all-to-all-done.3
  1081.0 42.2 %all_to_all.67 = bf16[16,8,768]{2,1,0:T(8,128)(2,1)S(1)} all-to-all(bf16[16,8,768]{2,1,0:T(8,128)(2,1)S(1)} %bitcast.277), channel_id=1, replica_groups=mesh['section'=16,'seq'=16] {'section'}, dimensions={0} | all-to-all | bytes 393216 | tf_op jit(solution)/shard_map/while/body/eval_jaxpr/all_to_all | solution.py:37
  1130.1 8.5 all-to-all-done.3
  1147.8 43.4 %all_to_all.67 = bf16[16,8,768]{2,1,0:T(8,128)(2,1)S(1)} all-to-all(bf16[16,8,768]{2,1,0:T(8,128)(2,1)S(1)} %bitcast.277), channel_id=1, replica_groups=mesh['section'=16,'seq'=16] {'section'}, dimensions={0} | all-to-all | bytes 393216 | tf_op jit(solution)/shard_map/while/body/eval_jaxpr/all_to_all | solution.py:37
  1198.1 8.5 all-to-all-done.3
  1208.1 9.0 collective-permute-start.7
  1218.0 45.1 %all_to_all.67 = bf16[16,8,768]{2,1,0:T(8,128)(2,1)S(1)} all-to-all(bf16[16,8,768]{2,1,0:T(8,128)(2,1)S(1)} %bitcast.277), channel_id=1, replica_groups=mesh['section'=16,'seq'=16] {'section'}, dimensions={0} | all-to-all | bytes 393216 | tf_op jit(solution)/shard_map/while/body/eval_jaxpr/all_to_all | solution.py:37
  1270.0 8.5 all-to-all-done.3
  1278.5 360.1 %while.82 = (s32[]{:T(128)}, bf16[128,768]{1,0:T(8,128)(2,1)S(1)}, f32[5,768,768]{2,1,0:T(8,128)}, f32[768]{0:T(1024)S(1)}, s32[]{:T(128)}, /*index=5*/pred[]{:T...) while((s32[]{:T(128)}, bf16[128,768]{1,0:T(8,128)(2,1)S(1)}, ...), condition=%wide.region_23.24_spmd, body=%wide.region_17.23_spmd.sunk | while | flops 1518029568 | bytes 81282136 | solution.py:196
  1278.7 8.5 collective-permute-start.10
  1371.5 139.2 %collective-permute-done.11 = bf16[128,768]{1,0:T(8,128)(2,1)S(1)} collective-permute-done((bf16[128,768]{1,0:T(8,128)(2,1)S(1)}, bf16[128,768]{1,0:T(8,128)(2,1)S(1)}, u32[]{:S(2)}, u32[]{:S(2)}) %collective-permute-start.11) | collective-permute-done | bytes 196640 | tf_op jit(solution)/shard_map/while/body/eval_jaxpr/ppermute | solution.py:27
  1521.2 28.2 %conditional.11 = (f32[5,768,768]{2,1,0:T(8,128)}, f32[768]{0:T(1024)S(1)}, bf16[128,768]{1,0:T(8,128)(2,1)S(1)}) conditional(s32[]{:T(128)} %convert_element_type.240, (f32[5,768,768]{2,1,0:T(8,128)}, f32[768]{0:T(1024)S(1)}) %tuple.226, (bf16[2,132,768]{2,1,0:T(8,128)(2,1)S(1)}, s32[]{:T(128)}, bf16[128,768]{1,0:T(8,128)(2,1)S(1)}, ...), branch_computations={%region_18.18_spmd, %region_19.22_spmd} | conditional | flops 1516831488 | bytes 79266456 | solution.py:177
  1530.8 13.9 add.389
  1565.5 28.2 %conditional.11 = (f32[5,768,768]{2,1,0:T(8,128)}, f32[768]{0:T(1024)S(1)}, bf16[128,768]{1,0:T(8,128)(2,1)S(1)}) conditional(s32[]{:T(128)} %convert_element_type.240, (f32[5,768,768]{2,1,0:T(8,128)}, f32[768]{0:T(1024)S(1)}) %tuple.226, (bf16[2,132,768]{2,1,0:T(8,128)(2,1)S(1)}, s32[]{:T(128)}, bf16[128,768]{1,0:T(8,128)(2,1)S(1)}, ...), branch_computations={%region_18.18_spmd, %region_19.22_spmd} | conditional | flops 1516831488 | bytes 79266456 | solution.py:177
  1575.1 13.9 add.389
  1609.8 27.8 %collective-permute-start.11 = (bf16[128,768]{1,0:T(8,128)(2,1)S(1)}, bf16[128,768]{1,0:T(8,128)(2,1)S(1)}, u32[]{:S(2)}, u32[]{:S(2)}) collective-permute-start(bf16[128,768]{1,0:T(8,128)(2,1)S(1)} %get-tuple-element.1869), channel_id=1, source_target_pairs={{16,0},{32,16},{48,32},{64,48},{80,64},{96,80},{112,96},{128,112},... | collective-permute-start | bytes 589832 | tf_op jit(solution)/shard_map/while/body/eval_jaxpr/ppermute | solution.py:27
  1648.0 39.0 %all-reduce = bf16[768]{0:T(1024)(128)(2,1)S(1)} all-reduce(bf16[768]{0:T(1024)(128)(2,1)S(1)} %convert_element_type.185), channel_id=3, replica_groups=mesh['section'=16,'seq'=16] {'seq'}, use_global_device_ids=true, to_apply=%region_25.26.clone | all-reduce | flops 768 | bytes 3072
  1687.6 98.0 %reduce-scatter.2.cloned.1.call-done = bf16[5,48,768]{2,1,0:T(8,128)(2,1)} async-done(((bf16[5,768,768]{2,1,0:T(8,128)(2,1)}), bf16[5,48,768]{2,1,0:T(8,128)(2,1)}) %reduce-scatter.2.cloned.1.call-update) | async-done | bytes 368656 | tf_op jit(solution)/shard_map/reduce_scatter | solution.py:201
  (624 shorter events, 674.9 us)
Async XLA Ops:
  7.2 1778.4 %reduce-scatter.2.cloned.1.call-start = ((), (), s32[]{:S(2)}) async-start(), calls=%async_computation.5 | async-start | bytes 6266880 | tf_op jit(solution)/shard_map/reduce_scatter | solution.py:201
  49.9 14.8 all-to-all-start.1
  54.3 10.4 collective-permute-start.2
  96.1 14.8 all-to-all-start.1
  100.5 10.5 collective-permute-start.2
  143.3 14.8 all-to-all-start.1
  147.6 10.5 collective-permute-start.2
  187.7 14.8 all-to-all-start.1
  192.0 10.5 collective-permute-start.2
  236.3 14.8 all-to-all-start.1
  240.6 10.5 collective-permute-start.2
  284.2 14.8 all-to-all-start.1
  288.6 10.5 collective-permute-start.2
  300.3 10.8 collective-permute-start
  301.6 10.2 collective-permute-start.1
  334.9 14.8 all-to-all-start.1
  339.3 10.5 collective-permute-start.2
  384.6 14.8 all-to-all-start.1
  388.9 10.5 collective-permute-start.2
  440.9 14.8 all-to-all-start.1
  445.2 10.5 collective-permute-start.2
  473.6 10.2 collective-permute-start.3
  493.7 10.2 collective-permute-start.3
  597.1 13.8 collective-permute-start.5
  709.1 14.8 all-to-all-start.3
  713.2 10.7 collective-permute-start.8
  777.5 14.8 all-to-all-start.3
  781.6 10.7 collective-permute-start.8
  846.8 14.8 all-to-all-start.3
  850.9 10.7 collective-permute-start.8
  916.0 14.8 all-to-all-start.3
  920.1 10.7 collective-permute-start.8
  930.9 10.1 collective-permute-start.6
  986.3 14.8 all-to-all-start.3
  990.4 10.7 collective-permute-start.8
  1001.3 10.2 collective-permute-start.6
  1055.7 14.8 all-to-all-start.3
  1059.8 10.7 collective-permute-start.8
  1123.8 14.8 all-to-all-start.3
  1127.9 10.7 collective-permute-start.8
  1191.9 14.8 all-to-all-start.3
  1196.0 10.7 collective-permute-start.8
  1206.8 10.3 collective-permute-start.6
  1263.7 14.8 all-to-all-start.3
  1267.8 10.7 collective-permute-start.8
  1278.7 9.9 collective-permute-start.10
  1369.6 141.1 %collective-permute-start.11 = (bf16[128,768]{1,0:T(8,128)(2,1)S(1)}, bf16[128,768]{1,0:T(8,128)(2,1)S(1)}, u32[]{:S(2)}, u32[]{:S(2)}) collective-permute-start(bf16[128,768]{1,0:T(8,128)(2,1)S(1)} %get-tuple-element.1869), channel_id=1, source_target_pairs={{16,0},{32,16},{48,32},{64,48},{80,64},{96,80},{112,96},{128,112},... | collective-permute-start | bytes 589832 | tf_op jit(solution)/shard_map/while/body/eval_jaxpr/ppermute | solution.py:27
  1609.8 28.9 %collective-permute-start.11 = (bf16[128,768]{1,0:T(8,128)(2,1)S(1)}, bf16[128,768]{1,0:T(8,128)(2,1)S(1)}, u32[]{:S(2)}, u32[]{:S(2)}) collective-permute-start(bf16[128,768]{1,0:T(8,128)(2,1)S(1)} %get-tuple-element.1869), channel_id=1, source_target_pairs={{16,0},{32,16},{48,32},{64,48},{80,64},{96,80},{112,96},{128,112},... | collective-permute-start | bytes 589832 | tf_op jit(solution)/shard_map/while/body/eval_jaxpr/ppermute | solution.py:27
  (82 other events, 634.5 us)
Sparse Core Ops, SparseCore 0:
  1646.2 139.2 reduce-scatter.1
where the time goes:
time: 1800 us; the launch traced here: 1790 us
  blocking collectives  664 us (37%)
  starting transfers between devices  502 us (28%)
  waiting for transfers between devices  474 us (26%)
  other arithmetic  66.9 us (4%)
  matrix products  44.1 us (2%)
  local copies, waits for them, and re-layouts  21.8 us (1%)
    all_to_all x18, blocking collectives, mirror(): lax.all_to_all(payload, 'section', split_axis=0, concat_axis=0, tiled=True)  625 us
    ppermute x35, starting transfers between devices, padded_2(): before = lax.ppermute(last, axis, up)  243 us
    ppermute x34, waiting for transfers between devices, passed_along(): return lax.ppermute(block, axis, route)  187 us
    ppermute x34, starting transfers between devices, passed_along(): return lax.ppermute(block, axis, route)  140 us
    all_to_all x18, waiting for transfers between devices, mirror(): lax.all_to_all(flipped, 'section', split_axis=0, concat_axis=0, tiled=True)  137 us
    reduce_scatter x1, waiting for transfers between devices, shards(): lax.psum_scatter(kernel_sum.astype(jnp.bfloat16), 'seq', scatter_dimensio...  98 us
    all_to_all x18, starting transfers between devices, mirror(): lax.all_to_all(flipped, 'section', split_axis=0, concat_axis=0, tiled=True)  74 us
    ppermute x35, starting transfers between devices, padded_2(): after = lax.ppermute(initial, axis, down)  45.2 us
  transfers between devices with their start and end apart: 123, of which 69 were waited for; matrix products, arithmetic and copies ran while one was open for 0% of the time, Pallas kernels for 0%

commit v1 on v0

v1 whole, which is shorter than its diff:
```python
import functools

import jax
import jax.numpy as jnp
from jax import lax
from jax.experimental import pallas as pl
from jax.experimental.pallas import tpu as pltpu
from jax.sharding import PartitionSpec as P

KERNEL = 5
STEM_K = 15
BASES = 4
C = 768
ROWS = 128
HALO = 8
WIDE = ROWS + 2 * HALO
PAD = WIDE + 16
STAGES = 8
BLOCKS = 16
SPAN = 4
TOKENS = BLOCKS * ROWS
AXES = ("section", "seq")
BF16 = jnp.bfloat16
F32 = jnp.float32
GELU_A = 0.7978845608028654
GELU_B = 0.044715
VMEM_SPEC = pl.BlockSpec(memory_space=pltpu.VMEM)
SMEM_SPEC = pl.BlockSpec(memory_space=pltpu.SMEM)
ANY_SPEC = pl.BlockSpec(memory_space=pl.ANY)


def place(stage, core, block):
    x, z = block // SPAN, block % SPAN
    column = x * SPAN + (SPAN - 1 - z if stage >= STAGES // 2 else z)
    return (2 * stage + core) * BLOCKS + column


def moved(array, source, target, shift=0):
    route = [
        (place(source, core, block), place(target, core, block + shift))
        for core in range(2)
        for block in range(BLOCKS)
        if 0 <= block + shift < BLOCKS
    ]
    return lax.ppermute(array, AXES, route)


def swapped(array):
    return lax.ppermute(array, "section", [(i, i ^ 1) for i in range(2 * STAGES)])


def turned_x(array, distance):
    route = [
        (x * SPAN + z, (x + distance) % SPAN * SPAN + z) for x in range(SPAN) for z in range(SPAN)
    ]
    return lax.ppermute(array, "seq", route)


def turned_z(array, distance):
    route = [
        (x * SPAN + z, x * SPAN + (z + distance) % SPAN) for x in range(SPAN) for z in range(SPAN)
    ]
    return lax.ppermute(array, "seq", route)


def hop(pieces, source, target):
    main, first, last = pieces
    return (
        moved(main, source, target),
        moved(last, source, target, 1),
        moved(first, source, target, -1),
    )


def params(mib):
    return pltpu.CompilerParams(vmem_limit_bytes=mib << 20)


def row_mask(block):
    row = lax.broadcasted_iota(jnp.int32, (WIDE, 1), 0) + (block * ROWS - HALO)
    return (row >= 0) & (row < TOKENS)


def normed(total):
    scale = lax.rsqrt(jnp.mean(total * total, axis=-1, keepdims=True) + 1e-06)
    return total * scale, scale


def forward_kernel(tick, info, *refs):
    skips = tick >= STAGES // 2
    last = tick == STAGES - 1
    refs = list(refs)
    main, left, right = refs[:3]
    refs = refs[3:]
    own_skip = refs.pop(0) if tick > STAGES // 2 else None
    skip_b = refs.pop(0) if skips else None
    filters, gains, whole, middle, act_a, act_b, sum_a, sum_b = refs[:8]
    out, first_rows, last_rows = refs[8:11] if not last else (None, None, None)
    pad = refs[-1]

    @pl.when(info[0] == tick)
    def _():
        keep = row_mask(info[1])
        whole[0:HALO, :] = left[...]
        whole[HALO : HALO + ROWS, :] = main[...]
        whole[HALO + ROWS : WIDE, :] = right[...]
        pad[0:8, :] = jnp.zeros((8, C), F32)
        pad[PAD - 8 : PAD, :] = jnp.zeros((8, C), F32)

        def activated(total, which, act):
            value, _ = normed(total)
            value = jax.nn.gelu(value * gains[which : which + 1, :])
            rounded = jnp.where(keep, value, 0.0).astype(BF16)
            act[...] = rounded
            pad[8 : 8 + WIDE, :] = rounded.astype(F32)

        def conv(total, which):
            for tap in range(KERNEL):
                start = 6 + tap
                total = total + jnp.dot(
                    pad[start : start + WIDE, :].astype(BF16),
                    filters[which, tap],
                    preferred_element_type=F32,
                )
            return total

        total = whole[...].astype(F32)
        if tick == STAGES // 2:
            total = total + total
        elif skips:
            total = total + own_skip[...].astype(F32)
        sum_a[...] = total
        activated(total, 0, act_a)
        value = conv(total, 0).astype(BF16)
        middle[...] = value
        total = value.astype(F32)
        if skips:
            total = total + skip_b[...].astype(F32)
        sum_b[...] = total
        activated(total, 1, act_b)
        if not last:
            value = conv(total, 1)
            out[...] = value[HALO : HALO + ROWS].astype(BF16)
            first_rows[...] = value[HALO : 2 * HALO].astype(BF16)
            last_rows[...] = value[ROWS : HALO + ROWS].astype(BF16)


def forward(tick, info, pieces, skip_a, skip_b, filters, gains):
    last = tick == STAGES - 1
    args = list(pieces)
    if skip_a is not None:
        args.append(skip_a)
    if skip_b is not None:
        args.append(skip_b)
    wide = jax.ShapeDtypeStruct((WIDE, C), BF16)
    total = jax.ShapeDtypeStruct((WIDE, C), F32)
    edge = jax.ShapeDtypeStruct((HALO, C), BF16)
    shapes = [wide, wide, wide, wide, total, total]
    if not last:
        shapes += [jax.ShapeDtypeStruct((ROWS, C), BF16), edge, edge]
    return pl.pallas_call(
        functools.partial(forward_kernel, tick),
        out_shape=shapes,
        in_specs=[SMEM_SPEC] + [VMEM_SPEC] * (len(args) + 2),
        out_specs=[VMEM_SPEC] * len(shapes),
        scratch_shapes=[pltpu.VMEM((PAD, C), F32)],
        compiler_params=params(16),
        name="forward_stage",
    )(info, *args, filters, gains)


def backward_kernel(tick, info, *refs):
    joined = tick < STAGES // 2
    refs = list(refs)
    main, left, right = refs[:3]
    refs = refs[3:]
    skip_a = refs.pop(0) if tick < STAGES // 2 - 1 else None
    skip_b = refs.pop(0) if joined else None
    sum_a, sum_b, filters, gains, whole, middle, grad_a, grad_b, gain_out = refs[:9]
    out, first_rows, last_rows = refs[9:12] if tick else (None, None, None)
    pad = refs[-1]

    @pl.when(info[0] == tick)
    def _():
        keep = row_mask(info[1])
        whole[0:HALO, :] = left[...]
        whole[HALO : HALO + ROWS, :] = main[...]
        whole[HALO + ROWS : WIDE, :] = right[...]
        pad[0:8, :] = jnp.zeros((8, C), F32)
        pad[PAD - 8 : PAD, :] = jnp.zeros((8, C), F32)

        def pull(grad, total_ref, which, grad_ref, last):
            grad_ref[...] = grad[HALO : HALO + ROWS].astype(BF16)
            pad[8 : 8 + WIDE, :] = grad
            grad_act = jnp.zeros((WIDE, C), F32)
            for tap in range(KERNEL):
                start = 10 - tap
                grad_act = grad_act + lax.dot_general(
                    pad[start : start + WIDE, :].astype(BF16),
                    filters[which, tap],
                    (((1,), (1,)), ((), ())),
                    preferred_element_type=F32,
                )
            total = total_ref[...]
            gain = gains[which : which + 1, :]
            value, scale = normed(total)
            inner = value * gain
            square = inner * inner
            tanh = jnp.tanh(GELU_A * (inner + GELU_B * (square * inner)))
            slope = 0.5 * (1.0 + tanh) + (0.5 * GELU_A) * inner * (1.0 - tanh * tanh) * (
                1.0 + (3.0 * GELU_B) * square
            )
            grad_inner = grad_act * slope
            product = (grad_inner * value)[HALO : HALO + ROWS]
            gain_out[which : which + 1, :] = jnp.sum(product, axis=0, keepdims=True)
            if last:
                return None
            grad_value = grad_inner * gain
            mean = jnp.mean(grad_value * value, axis=-1, keepdims=True)
            result = grad + scale * (grad_value - value * mean)
            return jnp.where(keep, result, 0.0).astype(BF16)

        grad = whole[...].astype(F32)
        if tick == STAGES // 2 - 1:
            grad = grad + grad
        elif joined:
            grad = grad + skip_a[...].astype(F32)
        grad = grad.astype(BF16).astype(F32)
        value = pull(grad, sum_b, 1, grad_b, False)
        middle[...] = value
        grad = value.astype(F32)
        if joined:
            grad = (grad + skip_b[...].astype(F32)).astype(BF16).astype(F32)
        value = pull(grad, sum_a, 0, grad_a, tick == 0)
        if tick:
            value = value.astype(F32)
            out[...] = value[HALO : HALO + ROWS].astype(BF16)
            first_rows[...] = value[HALO : 2 * HALO].astype(BF16)
            last_rows[...] = value[ROWS : HALO + ROWS].astype(BF16)


def backward(tick, info, pieces, skip_a, skip_b, sums, filters, gains):
    args = list(pieces)
    if skip_a is not None:
        args.append(skip_a)
    if skip_b is not None:
        args.append(skip_b)
    wide = jax.ShapeDtypeStruct((WIDE, C), BF16)
    own = jax.ShapeDtypeStruct((ROWS, C), BF16)
    edge = jax.ShapeDtypeStruct((HALO, C), BF16)
    shapes = [wide, wide, own, own, jax.ShapeDtypeStruct((2, C), F32)]
    if tick:
        shapes += [own, edge, edge]
    return pl.pallas_call(
        functools.partial(backward_kernel, tick),
        out_shape=shapes,
        in_specs=[SMEM_SPEC] + [VMEM_SPEC] * (len(args) + 4),
        out_specs=[VMEM_SPEC] * len(shapes),
        scratch_shapes=[pltpu.VMEM((PAD, C), F32)],
        compiler_params=params(16),
        name="backward_stage",
    )(info, *args, *sums, filters, gains)


def pair_kernel(info, own, other, pair, sems):
    core = info[2]
    copies = [
        pltpu.make_async_copy(own.at[0], pair.at[core], sems.at[0]),
        pltpu.make_async_copy(other.at[0], pair.at[1 - core], sems.at[1]),
    ]
    for copy in copies:
        copy.start()
    for copy in copies:
        copy.wait()


def paired(info, own, other):
    return pl.pallas_call(
        pair_kernel,
        out_shape=pltpu.VMEM((2, *own.shape[1:]), own.dtype),
        in_specs=[SMEM_SPEC, ANY_SPEC, ANY_SPEC],
        out_specs=VMEM_SPEC,
        scratch_shapes=[pltpu.SemaphoreType.DMA((2,))],
        compiler_params=params(14),
        name="weight_pair",
    )(info, own, other)


def product_kernel(rows_t, *refs):
    pieces, outs, total = refs[:SPAN], refs[SPAN : 2 * SPAN], refs[-1]
    count = 2 * ROWS
    for index, piece in enumerate(pieces):
        term = jnp.dot(
            rows_t[:, index * count : (index + 1) * count],
            piece[0:count, :],
            preferred_element_type=F32,
        )
        total[...] = term if index == 0 else total[...] + term
    gain = sum(piece[count : count + 8, :].astype(F32) for piece in pieces).astype(BF16)
    height = total.shape[0] // SPAN
    for index, out in enumerate(outs):
        out[0:height, :] = total[index * height : (index + 1) * height, :].astype(BF16)
        out[height : height + 8, :] = gain


def product(rows_t, pieces):
    height = rows_t.shape[0] // SPAN + 8
    return pl.pallas_call(
        product_kernel,
        out_shape=[jax.ShapeDtypeStruct((height, C), BF16)] * SPAN,
        in_specs=[VMEM_SPEC] * (1 + SPAN),
        out_specs=[VMEM_SPEC] * SPAN,
        scratch_shapes=[pltpu.VMEM((rows_t.shape[0], C), F32)],
        compiler_params=params(24),
        name="kernel_grad",
    )(rows_t, *pieces)


def chosen(stage, arrays):
    result = arrays[0]
    for index, array in enumerate(arrays[1:], 1):
        result = jnp.where(stage == index, array, result)
    return result


def shards(base_ids, stem_weight, conv_weight, block_gain, cotangent):
    section = lax.axis_index("section")
    column = lax.axis_index("seq")
    stage, core = section // 2, section % 2
    x, z = column // SPAN, column % SPAN
    late = stage >= STAGES // 2
    block = x * SPAN + jnp.where(late, SPAN - 1 - z, z)
    info = jnp.stack([stage, block, core]).astype(jnp.int32)

    filters = paired(info, conv_weight, swapped(conv_weight))
    other_gain = swapped(block_gain)
    gains = jnp.where(
        core == 0,
        jnp.concatenate([block_gain, other_gain], 0),
        jnp.concatenate([other_gain, block_gain], 0),
    )

    reach = HALO + STEM_K // 2
    ids = base_ids + 1
    ids = jnp.concatenate(
        [moved(ids[:, -reach:], 0, 0, 1), ids, moved(ids[:, :reach], 0, 0, -1)], 1
    )
    ids = lax.dynamic_index_in_dim(ids, core, 0, keepdims=False)
    letters = jnp.arange(1, BASES + 1, dtype=jnp.int32)
    onehot = jnp.concatenate(
        [ids[offset : offset + WIDE, None] == letters for offset in range(STEM_K)], axis=1
    ).astype(BF16)
    stem = jnp.dot(
        onehot, stem_weight.reshape(STEM_K * BASES, C), preferred_element_type=F32
    ).astype(BF16)

    last = STAGES - 1
    cot = lax.dynamic_index_in_dim(cotangent, core, 0, keepdims=False)

    def cot_moved(rows, shift):
        route = [
            ((2 * last + c) * BLOCKS + b, place(last, c, b + shift))
            for c in range(2)
            for b in range(BLOCKS)
            if 0 <= b + shift < BLOCKS
        ]
        return lax.ppermute(rows, AXES, route)

    cot_pieces = (
        cot_moved(cot, 0),
        cot_moved(cot[ROWS - HALO :], 1),
        cot_moved(cot[:HALO], -1),
    )

    pieces = (stem[HALO : HALO + ROWS], stem[:HALO], stem[HALO + ROWS :])
    skip_whole, skip_middle, sums, acts = {}, {}, [], []
    half = STAGES // 2
    for tick in range(STAGES):
        results = forward(
            tick,
            info,
            pieces,
            skip_whole.get(tick),
            skip_middle.get(tick),
            filters,
            gains,
        )
        whole, middle, act_a, act_b, sum_a, sum_b = results[:6]
        sums.append((sum_a, sum_b))
        acts.append((act_a, act_b))
        if tick < last:
            pieces = hop(results[6:], tick, tick + 1)
        if tick < half:
            skip_middle[last - tick] = moved(middle, tick, last - tick)
            if tick:
                skip_whole[STAGES - tick] = moved(whole, tick, STAGES - tick)

    keep = chosen(stage, [jnp.where(core == 0, a, b) for a, b in acts])
    give = chosen(stage, [jnp.where(core == 0, b, a) for a, b in acts])
    both = jnp.stack([keep, swapped(give)])
    width = C // SPAN
    split = both.reshape(2, WIDE, SPAN, width).transpose(2, 0, 1, 3)

    def slice_for(distance):
        return lax.dynamic_index_in_dim(split, (x + distance) % SPAN, 0, keepdims=False)

    gathered = jnp.stack(
        [slice_for(0)] + [turned_x(slice_for(d), d) for d in range(1, SPAN)]
    )
    taps = jnp.stack(
        [gathered[:, :, HALO - 2 + k : HALO - 2 + k + ROWS] for k in range(KERNEL)]
    )
    share = width // SPAN
    rows_t = taps.reshape(KERNEL, SPAN * 2 * ROWS, SPAN, share).transpose(2, 0, 3, 1)
    rows_t = jnp.concatenate(
        [
            lax.dynamic_index_in_dim(rows_t, (z + d) % SPAN, 0, keepdims=False)
            for d in range(SPAN)
        ],
        0,
    ).reshape(SPAN * KERNEL * share, SPAN * 2 * ROWS)

    pieces = cot_pieces
    skip_whole, skip_middle, grads, gain_parts = {}, {}, [None] * STAGES, [None] * STAGES
    for tick in reversed(range(STAGES)):
        results = backward(
            tick,
            info,
            pieces,
            skip_whole.get(tick),
            skip_middle.get(tick),
            sums[tick],
            filters,
            gains,
        )
        whole, middle, grad_a, grad_b, gain_part = results[:5]
        grads[tick] = (grad_a, grad_b)
        gain_parts[tick] = gain_part
        if tick:
            pieces = hop(results[5:], tick, tick - 1)
        if tick >= half:
            skip_middle[last - tick] = moved(middle, tick, last - tick)
            if tick < last:
                skip_whole[last - 1 - tick] = moved(whole, tick, last - 1 - tick)

    gain_part = chosen(stage, gain_parts)
    keep = chosen(stage, [jnp.where(core == 0, a, b) for a, b in grads])
    give = chosen(stage, [jnp.where(core == 0, b, a) for a, b in grads])
    keep_gain = jnp.where(core == 0, gain_part[0:1], gain_part[1:2])
    give_gain = jnp.where(core == 0, gain_part[1:2], gain_part[0:1])
    none = jnp.zeros((7, C), BF16)
    got = swapped(jnp.concatenate([give, give_gain.astype(BF16), none], 0))
    total_gain = keep_gain + got[ROWS : ROWS + 1].astype(F32)
    both = jnp.concatenate([keep, got[:ROWS], total_gain.astype(BF16), none], 0)
    parts = product(rows_t, [both] + [turned_x(both, d) for d in range(1, SPAN)])
    total = parts[0].astype(F32)
    for d in range(1, SPAN):
        total = total + turned_z(parts[d], d).astype(F32)
    height = KERNEL * share
    kernel_grad = total[:height].astype(BF16).reshape(1, KERNEL, share, C)
    gain_grad = lax.dynamic_slice_in_dim(total[height], column * share, share)
    return kernel_grad, gain_grad[None]


def solution(mesh):
    placed = (
        P(None, "seq"),
        P(),
        P("section", None, None, None),
        P("section", None),
        P(None, "seq", None),
    )
    return jax.shard_map(
        shards,
        mesh=mesh,
        in_specs=placed,
        out_specs=(P("section", None, "seq", None), P("section", "seq")),
        check_vma=False,
    )
```

time: 1800 us -> 769 us (0.43)
  blocking collectives: 664 us -> 0 us
  waiting for transfers between devices: 474 us -> 33.8 us
  starting transfers between devices: 502 us -> 586 us
  local copies, waits for them, and re-layouts: 21.8 us -> 91.2 us
  other arithmetic: 66.9 us -> 6.04 us
  matrix products: 44.1 us -> 0.19 us
  Pallas kernels: 0 us -> 38.8 us
    all_to_all x18 -> x0, blocking collectives: 625 us -> none  [mirror(): lax.all_to_all(payload, 'section', split_axis=0, concat_axis=0, tiled=True)]
    ppermute x104 -> x74, waiting for transfers between devices: 239 us -> 33.8 us  [the longest x3 16.5 us: turned_z(): return lax.ppermute(array, 'seq', route)]
    ppermute x104 -> x74, starting transfers between devices: 428 us -> 586 us  [the longest x58 512 us: moved(): return lax.ppermute(array, AXES, route)]
    all_to_all x18 -> x0, waiting for transfers between devices: 137 us -> none  [mirror(): lax.all_to_all(flipped, 'section', split_axis=0, concat_axis=0, tiled=True)]
    reduce_scatter x1 -> x0, waiting for transfers between devices: 98 us -> none  [shards(): lax.psum_scatter(kernel_sum.astype(jnp.bfloat16), 'seq', scatter_dimensio...]
    all_to_all x18 -> x0, starting transfers between devices: 74 us -> none  [mirror(): lax.all_to_all(flipped, 'section', split_axis=0, concat_axis=0, tiled=True)]
    unnamed x7 -> x135, local copies, waits for them, and re-layouts: 1.24 us -> 58.8 us
    dot_general x31 -> x1, matrix products: 44.1 us -> 0.19 us  [shards(): jnp.dot(onehot, stem_weight.reshape(STEM_K * BASES, C), preferred_element...]
  transfers between devices with their start and end apart: 123 -> 74, of which waited for: 69 -> 8; matrix products, arithmetic and copies ran while one was open for 0% -> 5% of each run, Pallas kernels for 0% -> 2%
where the time goes in v1:
time: 769 us; the launch traced here: 759 us
  starting transfers between devices  586 us (76%)
  local copies, waits for them, and re-layouts  91.2 us (12%)
  Pallas kernels  38.8 us (5%)
  waiting for transfers between devices  33.8 us (4%)
    ppermute x58, starting transfers between devices, moved(): return lax.ppermute(array, AXES, route)  512 us
    unnamed x135, local copies, waits for them, and re-layouts  58.8 us
    ppermute x3, starting transfers between devices, turned_z(): return lax.ppermute(array, 'seq', route)  32 us
    pallas_call x8, Pallas kernels, backward(): pl.pallas_call(functools.partial(backward_kernel, tick), out_shape=shapes...  19.5 us
    ppermute x3, waiting for transfers between devices, turned_z(): return lax.ppermute(array, 'seq', route)  16.5 us
    ppermute x3, starting transfers between devices, cot_moved(): return lax.ppermute(rows, AXES, route)  16.3 us
    ppermute x4, starting transfers between devices, swapped(): lax.ppermute(array, 'section', [(i, i ^ 1) for i in range(2 * STAGES)])  15.9 us
  transfers between devices with their start and end apart: 74, of which 8 were waited for; matrix products, arithmetic and copies ran while one was open for 5% of the time, Pallas kernels for 2%

profile of v1, /device:TPU:1, one launch (start us, length us, event | category | flops | bytes accessed | tf_op | source)
XLA Modules:
  0.0 758.6 jit_solution(15622614922381988262)
XLA Ops:
  7.8 9.0 %collective-permute-start.3 = (f32[1,768]{1,0:T(1,128)}, f32[1,768]{1,0:T(1,128)S(1)}, u32[]{:S(2)}, u32[]{:S(2)}) collective-permute-start(f32[1,768]{1,0:T(1,128)} %param.8), channel_id=1, source_target_pairs={{0,16},{16,0},{32,48},{48,32},{64,80},{80,64},{96,112},{112,96},{1... | collective-permute-start | bytes 9224 | tf_op jit(solution)/shard_map/ppermute | solution.py:49
  23.1 3.8 weight_pair.1.refs_3_.refs_4_.refs_5_.refs_6_.refs_7_
  26.9 5.5 forward_stage.8
  33.2 9.5 %collective-permute-start.4 = (bf16[128,768]{1,0:T(8,128)(2,1)S(1)}, bf16[128,768]{1,0:T(8,128)(2,1)S(1)}, u32[]{:S(2)}, u32[]{:S(2)}) collective-permute-start(bf16[128,768]{1,0:T(8,128)(2,1)S(1)} %get-tuple-element.118), channel_id=1, source_target_pairs={{0,32},{1,33},{2,34},{3,35},{4,36},{5,37},{6,38},{7,39},{8,40},{9,... | collective-permute-start | bytes 589832 | tf_op jit(solution)/shard_map/ppermute | solution.py:45
  42.7 3.7 collective-permute-start.5
  49.3 18.0 %collective-permute-start.7 = (bf16[128,768]{1,0:T(8,128)(2,1)S(1)}, bf16[128,768]{1,0:T(8,128)(2,1)S(1)}, u32[]{:S(2)}, u32[]{:S(2)}) collective-permute-start(bf16[128,768]{1,0:T(8,128)(2,1)S(1)} %get-tuple-element.121), channel_id=1, source_target_pairs={{32,64},{33,65},{34,66},{35,67},{36,68},{37,69},{38,70},{39,71},{4... | collective-permute-start | bytes 589832 | tf_op jit(solution)/shard_map/ppermute | solution.py:45
  70.8 23.4 %collective-permute-start.10 = (bf16[128,768]{1,0:T(8,128)(2,1)S(1)}, bf16[128,768]{1,0:T(8,128)(2,1)S(1)}, u32[]{:S(2)}, u32[]{:S(2)}) collective-permute-start(bf16[128,768]{1,0:T(8,128)(2,1)S(1)} %get-tuple-element.124), channel_id=1, source_target_pairs={{64,96},{65,97},{66,98},{67,99},{68,100},{69,101},{70,102},{71,103... | collective-permute-start | bytes 589832 | tf_op jit(solution)/shard_map/ppermute | solution.py:45
  97.8 23.0 %collective-permute-start.16 = (bf16[144,768]{1,0:T(8,128)(2,1)S(1)}, bf16[144,768]{1,0:T(8,128)(2,1)S(1)}, u32[]{:S(2)}, u32[]{:S(2)}) collective-permute-start(bf16[144,768]{1,0:T(8,128)(2,1)S(1)} %get-tuple-element.130), channel_id=1, source_target_pairs={{96,131},{97,130},{98,129},{99,128},{100,135},{101,134},{102,133},... | collective-permute-start | bytes 663560 | tf_op jit(solution)/shard_map/ppermute | solution.py:45
  120.7 12.5 %collective-permute-start.13 = (bf16[128,768]{1,0:T(8,128)(2,1)S(1)}, bf16[128,768]{1,0:T(8,128)(2,1)S(1)}, u32[]{:S(2)}, u32[]{:S(2)}) collective-permute-start(bf16[128,768]{1,0:T(8,128)(2,1)S(1)} %get-tuple-element.127), channel_id=1, source_target_pairs={{96,131},{97,130},{98,129},{99,128},{100,135},{101,134},{102,133},... | collective-permute-start | bytes 589832 | tf_op jit(solution)/shard_map/ppermute | solution.py:45
  133.2 12.5 %collective-permute-start.21 = (bf16[144,768]{1,0:T(8,128)(2,1)S(1)}, bf16[144,768]{1,0:T(8,128)(2,1)S(1)}, u32[]{:S(2)}, u32[]{:S(2)}) collective-permute-start(bf16[144,768]{1,0:T(8,128)(2,1)S(1)} %get-tuple-element.135), channel_id=1, source_target_pairs={{64,163},{65,162},{66,161},{67,160},{68,167},{69,166},{70,165},{71... | collective-permute-start | bytes 663560 | tf_op jit(solution)/shard_map/ppermute | solution.py:45
  145.7 12.5 %collective-permute-start.20 = (bf16[144,768]{1,0:T(8,128)(2,1)S(1)}, bf16[144,768]{1,0:T(8,128)(2,1)S(1)}, u32[]{:S(2)}, u32[]{:S(2)}) collective-permute-start(bf16[144,768]{1,0:T(8,128)(2,1)S(1)} %get-tuple-element.134), channel_id=1, source_target_pairs={{96,163},{97,162},{98,161},{99,160},{100,167},{101,166},{102,165},... | collective-permute-start | bytes 663560 | tf_op jit(solution)/shard_map/ppermute | solution.py:45
  162.5 36.2 %collective-permute-start.17 = (bf16[128,768]{1,0:T(8,128)(2,1)S(1)}, bf16[128,768]{1,0:T(8,128)(2,1)S(1)}, u32[]{:S(2)}, u32[]{:S(2)}) collective-permute-start(bf16[128,768]{1,0:T(8,128)(2,1)S(1)} %get-tuple-element.131), channel_id=1, source_target_pairs={{131,163},{130,162},{129,161},{128,160},{135,167},{134,166},{133,1... | collective-permute-start | bytes 589832 | tf_op jit(solution)/shard_map/ppermute | solution.py:45
  198.7 12.5 %collective-permute-start.26 = (bf16[144,768]{1,0:T(8,128)(2,1)S(1)}, bf16[144,768]{1,0:T(8,128)(2,1)S(1)}, u32[]{:S(2)}, u32[]{:S(2)}) collective-permute-start(bf16[144,768]{1,0:T(8,128)(2,1)S(1)} %get-tuple-element.140), channel_id=1, source_target_pairs={{32,195},{33,194},{34,193},{35,192},{36,199},{37,198},{38,197},{39... | collective-permute-start | bytes 663560 | tf_op jit(solution)/shard_map/ppermute | solution.py:45
  211.2 12.5 %collective-permute-start.25 = (bf16[144,768]{1,0:T(8,128)(2,1)S(1)}, bf16[144,768]{1,0:T(8,128)(2,1)S(1)}, u32[]{:S(2)}, u32[]{:S(2)}) collective-permute-start(bf16[144,768]{1,0:T(8,128)(2,1)S(1)} %get-tuple-element.139), channel_id=1, source_target_pairs={{64,195},{65,194},{66,193},{67,192},{68,199},{69,198},{70,197},{71... | collective-permute-start | bytes 663560 | tf_op jit(solution)/shard_map/ppermute | solution.py:45
  227.1 24.2 %collective-permute-start.22 = (bf16[128,768]{1,0:T(8,128)(2,1)S(1)}, bf16[128,768]{1,0:T(8,128)(2,1)S(1)}, u32[]{:S(2)}, u32[]{:S(2)}) collective-permute-start(bf16[128,768]{1,0:T(8,128)(2,1)S(1)} %get-tuple-element.136), channel_id=1, source_target_pairs={{163,195},{162,194},{161,193},{160,192},{167,199},{166,198},{165,1... | collective-permute-start | bytes 589832 | tf_op jit(solution)/shard_map/ppermute | solution.py:45
  252.7 16.4 %collective-permute-start.31 = (bf16[144,768]{1,0:T(8,128)(2,1)}, bf16[144,768]{1,0:T(8,128)(2,1)S(1)}, u32[]{:S(2)}, u32[]{:S(2)}) collective-permute-start(bf16[144,768]{1,0:T(8,128)(2,1)} %get-tuple-element.145), channel_id=1, source_target_pairs={{0,227},{1,226},{2,225},{3,224},{4,231},{5,230},{6,229},{7,228},{8... | collective-permute-start | bytes 663560 | tf_op jit(solution)/shard_map/ppermute | solution.py:45
  269.1 12.0 %collective-permute-start.30 = (bf16[144,768]{1,0:T(8,128)(2,1)}, bf16[144,768]{1,0:T(8,128)(2,1)S(1)}, u32[]{:S(2)}, u32[]{:S(2)}) collective-permute-start(bf16[144,768]{1,0:T(8,128)(2,1)} %get-tuple-element.144), channel_id=1, source_target_pairs={{32,227},{33,226},{34,225},{35,224},{36,231},{37,230},{38,229},{39... | collective-permute-start | bytes 663560 | tf_op jit(solution)/shard_map/ppermute | solution.py:45
  285.5 17.3 %collective-permute-start.27 = (bf16[128,768]{1,0:T(8,128)(2,1)}, bf16[128,768]{1,0:T(8,128)(2,1)}, u32[]{:S(2)}, u32[]{:S(2)}) collective-permute-start(bf16[128,768]{1,0:T(8,128)(2,1)} %get-tuple-element.141), channel_id=1, source_target_pairs={{195,227},{194,226},{193,225},{192,224},{199,231},{198,230},{197,2... | collective-permute-start | bytes 589832 | tf_op jit(solution)/shard_map/ppermute | solution.py:45
  303.5 13.8 %collective-permute-start.36 = (bf16[128,768]{1,0:T(8,128)(2,1)}, bf16[128,768]{1,0:T(8,128)(2,1)}, u32[]{:S(2)}, u32[]{:S(2)}) collective-permute-start(bf16[128,768]{1,0:T(8,128)(2,1)} %dynamic-slice_bitcast_fusion.4), channel_id=1, source_target_pairs={{224,227},{225,226},{226,225},{227,224},{228,231},{229,230},{230,2... | collective-permute-start | bytes 589832 | tf_op jit(solution)/shard_map/ppermute | solution.py:367
  323.6 4.4 copy-done.1
  332.1 27.5 %collective-permute-start.39 = (bf16[128,768]{1,0:T(8,128)(2,1)}, bf16[128,768]{1,0:T(8,128)(2,1)}, u32[]{:S(2)}, u32[]{:S(2)}) collective-permute-start(bf16[128,768]{1,0:T(8,128)(2,1)} %get-tuple-element.166), channel_id=1, source_target_pairs={{227,195},{226,194},{225,193},{224,192},{231,199},{230,198},{229,1... | collective-permute-start | bytes 589832 | tf_op jit(solution)/shard_map/ppermute | solution.py:45
  366.1 4.3 copy-done.2
  373.9 22.7 %collective-permute-start.42 = (bf16[128,768]{1,0:T(8,128)(2,1)S(1)}, bf16[128,768]{1,0:T(8,128)(2,1)S(1)}, u32[]{:S(2)}, u32[]{:S(2)}) collective-permute-start(bf16[128,768]{1,0:T(8,128)(2,1)S(1)} %get-tuple-element.173), channel_id=1, source_target_pairs={{195,163},{194,162},{193,161},{192,160},{199,167},{198,166},{197,1... | collective-permute-start | bytes 589832 | tf_op jit(solution)/shard_map/ppermute | solution.py:45
  399.3 4.3 copy-done.3
  404.9 25.7 %collective-permute-start.45 = (bf16[128,768]{1,0:T(8,128)(2,1)S(1)}, bf16[128,768]{1,0:T(8,128)(2,1)S(1)}, u32[]{:S(2)}, u32[]{:S(2)}) collective-permute-start(bf16[128,768]{1,0:T(8,128)(2,1)S(1)} %get-tuple-element.180), channel_id=1, source_target_pairs={{163,131},{162,130},{161,129},{160,128},{167,135},{166,134},{165,1... | collective-permute-start | bytes 589832 | tf_op jit(solution)/shard_map/ppermute | solution.py:45
  440.5 25.5 %collective-permute-start.51 = (bf16[144,768]{1,0:T(8,128)(2,1)}, bf16[144,768]{1,0:T(8,128)(2,1)S(1)}, u32[]{:S(2)}, u32[]{:S(2)}) collective-permute-start(bf16[144,768]{1,0:T(8,128)(2,1)} %get-tuple-element.190), channel_id=1, source_target_pairs={{131,96},{130,97},{129,98},{128,99},{135,100},{134,101},{133,102},... | collective-permute-start | bytes 663560 | tf_op jit(solution)/shard_map/ppermute | solution.py:45
  466.1 12.5 %collective-permute-start.48 = (bf16[128,768]{1,0:T(8,128)(2,1)}, bf16[128,768]{1,0:T(8,128)(2,1)S(1)}, u32[]{:S(2)}, u32[]{:S(2)}) collective-permute-start(bf16[128,768]{1,0:T(8,128)(2,1)} %get-tuple-element.187), channel_id=1, source_target_pairs={{131,96},{130,97},{129,98},{128,99},{135,100},{134,101},{133,102},... | collective-permute-start | bytes 589832 | tf_op jit(solution)/shard_map/ppermute | solution.py:45
  481.1 14.3 %collective-permute-start.56 = (bf16[144,768]{1,0:T(8,128)(2,1)}, bf16[144,768]{1,0:T(8,128)(2,1)S(1)}, u32[]{:S(2)}, u32[]{:S(2)}) collective-permute-start(bf16[144,768]{1,0:T(8,128)(2,1)} %copy-done.55), channel_id=1, source_target_pairs={{163,64},{162,65},{161,66},{160,67},{167,68},{166,69},{165,70},{16... | collective-permute-start | bytes 663560 | tf_op jit(solution)/shard_map/ppermute | solution.py:45
  495.5 13.2 %collective-permute-start.55 = (bf16[144,768]{1,0:T(8,128)(2,1)}, bf16[144,768]{1,0:T(8,128)(2,1)}, u32[]{:S(2)}, u32[]{:S(2)}) collective-permute-start(bf16[144,768]{1,0:T(8,128)(2,1)} %copy-done.56), channel_id=1, source_target_pairs={{131,64},{130,65},{129,66},{128,67},{135,68},{134,69},{133,70},{13... | collective-permute-start | bytes 663560 | tf_op jit(solution)/shard_map/ppermute | solution.py:45
  509.4 4.3 copy-done.4
  516.6 16.8 %collective-permute-start.52 = (bf16[128,768]{1,0:T(8,128)(2,1)}, bf16[128,768]{1,0:T(8,128)(2,1)S(1)}, u32[]{:S(2)}, u32[]{:S(2)}) collective-permute-start(bf16[128,768]{1,0:T(8,128)(2,1)} %get-tuple-element.195), channel_id=1, source_target_pairs={{96,64},{97,65},{98,66},{99,67},{100,68},{101,69},{102,70},{103,71... | collective-permute-start | bytes 589832 | tf_op jit(solution)/shard_map/ppermute | solution.py:45
  544.5 13.2 %collective-permute-start.61 = (bf16[144,768]{1,0:T(8,128)(2,1)}, bf16[144,768]{1,0:T(8,128)(2,1)}, u32[]{:S(2)}, u32[]{:S(2)}) collective-permute-start(bf16[144,768]{1,0:T(8,128)(2,1)} %copy-done.53), channel_id=1, source_target_pairs={{195,32},{194,33},{193,34},{192,35},{199,36},{198,37},{197,38},{19... | collective-permute-start | bytes 663560 | tf_op jit(solution)/shard_map/ppermute | solution.py:45
  557.7 13.8 %collective-permute-start.60 = (bf16[144,768]{1,0:T(8,128)(2,1)}, bf16[144,768]{1,0:T(8,128)(2,1)}, u32[]{:S(2)}, u32[]{:S(2)}) collective-permute-start(bf16[144,768]{1,0:T(8,128)(2,1)} %copy-done.54), channel_id=1, source_target_pairs={{163,32},{162,33},{161,34},{160,35},{167,36},{166,37},{165,38},{16... | collective-permute-start | bytes 663560 | tf_op jit(solution)/shard_map/ppermute | solution.py:45
  572.2 4.4 copy-done.5
  579.5 17.0 %collective-permute-start.57 = (bf16[128,768]{1,0:T(8,128)(2,1)}, bf16[128,768]{1,0:T(8,128)(2,1)S(1)}, u32[]{:S(2)}, u32[]{:S(2)}) collective-permute-start(bf16[128,768]{1,0:T(8,128)(2,1)} %get-tuple-element.204), channel_id=1, source_target_pairs={{64,32},{65,33},{66,34},{67,35},{68,36},{69,37},{70,38},{71,39},{7... | collective-permute-start | bytes 589832 | tf_op jit(solution)/shard_map/ppermute | solution.py:45
  607.6 12.5 %collective-permute-start.66 = (bf16[144,768]{1,0:T(8,128)(2,1)}, bf16[144,768]{1,0:T(8,128)(2,1)S(1)}, u32[]{:S(2)}, u32[]{:S(2)}) collective-permute-start(bf16[144,768]{1,0:T(8,128)(2,1)} %copy-done.51), channel_id=1, source_target_pairs={{227,0},{226,1},{225,2},{224,3},{231,4},{230,5},{229,6},{228,7},{2... | collective-permute-start | bytes 663560 | tf_op jit(solution)/shard_map/ppermute | solution.py:45
  620.1 12.9 %collective-permute-start.65 = (bf16[144,768]{1,0:T(8,128)(2,1)}, bf16[144,768]{1,0:T(8,128)(2,1)}, u32[]{:S(2)}, u32[]{:S(2)}) collective-permute-start(bf16[144,768]{1,0:T(8,128)(2,1)} %copy-done.52), channel_id=1, source_target_pairs={{195,0},{194,1},{193,2},{192,3},{199,4},{198,5},{197,6},{196,7},{2... | collective-permute-start | bytes 663560 | tf_op jit(solution)/shard_map/ppermute | solution.py:45
  633.7 4.3 copy-done.6
  642.0 16.2 %collective-permute-start.62 = (bf16[128,768]{1,0:T(8,128)(2,1)}, bf16[128,768]{1,0:T(8,128)(2,1)}, u32[]{:S(2)}, u32[]{:S(2)}) collective-permute-start(bf16[128,768]{1,0:T(8,128)(2,1)} %get-tuple-element.213), channel_id=1, source_target_pairs={{32,0},{33,1},{34,2},{35,3},{36,4},{37,5},{38,6},{39,7},{40,8},{41... | collective-permute-start | bytes 589832 | tf_op jit(solution)/shard_map/ppermute | solution.py:45
  667.1 4.3 copy-done.7
  672.5 8.9 %backward_stage.15 = (bf16[144,768]{1,0:T(8,128)(2,1)}, bf16[144,768]{1,0:T(8,128)(2,1)}, bf16[128,768]{1,0:T(8,128)(2,1)S(1)}, bf16[128,768]{1,0:T(8,128)(2,1)S(1)}, f32[2,768]{1,0:T(2,128)S(1)}) custom-call(s32[3]{0:T(128)S(1)} %pad_add_fusion.info, bf16[128,768]{1,0:T(8,128)(2,1)} %collective-permute-done.62.refs_0_, ...), custom_call_target="tpu_custom_call" | custom-call | tf_op jit(solution)/shard_map/backward_stage/pallas_call | solution.py:254
  692.2 4.5 collective-permute-done.68.refs_1_
  696.7 9.7 %collective-permute-done.69.refs_2_ = bf16[264,768]{1,0:T(8,128)(2,1)S(1)} collective-permute-done((bf16[264,768]{1,0:T(8,128)(2,1)S(1)}, bf16[264,768]{1,0:T(8,128)(2,1)S(1)}, u32[]{:S(2)}, u32[]{:S(2)}) %collective-permute-start.69) | collective-permute-done | bytes 405536 | tf_op jit(solution)/shard_map/ppermute | solution.py:56
  708.1 8.3 %collective-permute-start.71 = (bf16[248,768]{1,0:T(8,128)(2,1)S(1)}, bf16[248,768]{1,0:T(8,128)(2,1)S(1)}, u32[]{:S(2)}, u32[]{:S(2)}) collective-permute-start(bf16[248,768]{1,0:T(8,128)(2,1)S(1)} %get-tuple-element.231), channel_id=1, source_target_pairs={{0,1},{1,2},{2,3},{3,0},{4,5},{5,6},{6,7},{7,4},{8,9},{9,10},{10,1... | collective-permute-start | bytes 1142792 | tf_op jit(solution)/shard_map/ppermute | solution.py:63
  716.4 11.8 %collective-permute-start.72 = (bf16[248,768]{1,0:T(8,128)(2,1)S(1)}, bf16[248,768]{1,0:T(8,128)(2,1)S(1)}, u32[]{:S(2)}, u32[]{:S(2)}) collective-permute-start(bf16[248,768]{1,0:T(8,128)(2,1)S(1)} %get-tuple-element.232), channel_id=1, source_target_pairs={{0,2},{1,3},{2,0},{3,1},{4,6},{5,7},{6,4},{7,5},{8,10},{9,11},{10,... | collective-permute-start | bytes 1142792 | tf_op jit(solution)/shard_map/ppermute | solution.py:63
  728.2 11.8 %collective-permute-start.73 = (bf16[248,768]{1,0:T(8,128)(2,1)S(1)}, bf16[248,768]{1,0:T(8,128)(2,1)S(1)}, u32[]{:S(2)}, u32[]{:S(2)}) collective-permute-start(bf16[248,768]{1,0:T(8,128)(2,1)S(1)} %get-tuple-element.233), channel_id=1, source_target_pairs={{0,3},{1,0},{2,1},{3,2},{4,7},{5,4},{6,5},{7,6},{8,11},{9,8},{10,9... | collective-permute-start | bytes 1142792 | tf_op jit(solution)/shard_map/ppermute | solution.py:63
  740.1 8.0 %collective-permute-done.72 = bf16[248,768]{1,0:T(8,128)(2,1)S(1)} collective-permute-done((bf16[248,768]{1,0:T(8,128)(2,1)S(1)}, bf16[248,768]{1,0:T(8,128)(2,1)S(1)}, u32[]{:S(2)}, u32[]{:S(2)}) %collective-permute-start.72) | collective-permute-done | bytes 380960 | tf_op jit(solution)/shard_map/ppermute | solution.py:63
  748.1 8.5 %collective-permute-done.73 = bf16[248,768]{1,0:T(8,128)(2,1)S(1)} collective-permute-done((bf16[248,768]{1,0:T(8,128)(2,1)S(1)}, bf16[248,768]{1,0:T(8,128)(2,1)S(1)}, u32[]{:S(2)}, u32[]{:S(2)}) %collective-permute-start.73) | collective-permute-done | bytes 380960 | tf_op jit(solution)/shard_map/ppermute | solution.py:63
  (302 shorter events, 132.5 us)
Async XLA Ops:
  0.6 19.8 %collective-permute-start.2 = (bf16[1,5,768,768]{3,2,1,0:T(8,128)(2,1)}, bf16[1,5,768,768]{3,2,1,0:T(8,128)(2,1)}, u32[]{:S(2)}, u32[]{:S(2)}) collective-permute-start(bf16[1,5,768,768]{3,2,1,0:T(8,128)(2,1)} %own.1), channel_id=1, source_target_pairs={{0,16},{16,0},{32,48},{48,32},{64,80},{80,64},{96,112},{112,96},{1... | collective-permute-start | bytes 17694728 | tf_op jit(solution)/shard_map/ppermute | solution.py:49
  4.7 13.1 %collective-permute-start = (s32[2,15]{1,0:T(2,128)S(1)}, s32[2,15]{1,0:T(2,128)S(1)}, u32[]{:S(2)}, u32[]{:S(2)}) collective-permute-start(s32[2,15]{1,0:T(2,128)S(1)} %get-tuple-element.266), channel_id=1, source_target_pairs={{0,1},{1,2},{2,3},{3,4},{4,5},{5,6},{6,7},{7,8},{8,9},{9,10},{10,1... | collective-permute-start | bytes 368 | tf_op jit(solution)/shard_map/ppermute | solution.py:45
  33.2 14.1 %collective-permute-start.4 = (bf16[128,768]{1,0:T(8,128)(2,1)S(1)}, bf16[128,768]{1,0:T(8,128)(2,1)S(1)}, u32[]{:S(2)}, u32[]{:S(2)}) collective-permute-start(bf16[128,768]{1,0:T(8,128)(2,1)S(1)} %get-tuple-element.118), channel_id=1, source_target_pairs={{0,32},{1,33},{2,34},{3,35},{4,36},{5,37},{6,38},{7,39},{8,40},{9,... | collective-permute-start | bytes 589832 | tf_op jit(solution)/shard_map/ppermute | solution.py:45
  49.3 19.4 %collective-permute-start.7 = (bf16[128,768]{1,0:T(8,128)(2,1)S(1)}, bf16[128,768]{1,0:T(8,128)(2,1)S(1)}, u32[]{:S(2)}, u32[]{:S(2)}) collective-permute-start(bf16[128,768]{1,0:T(8,128)(2,1)S(1)} %get-tuple-element.121), channel_id=1, source_target_pairs={{32,64},{33,65},{34,66},{35,67},{36,68},{37,69},{38,70},{39,71},{4... | collective-permute-start | bytes 589832 | tf_op jit(solution)/shard_map/ppermute | solution.py:45
  70.8 24.9 %collective-permute-start.10 = (bf16[128,768]{1,0:T(8,128)(2,1)S(1)}, bf16[128,768]{1,0:T(8,128)(2,1)S(1)}, u32[]{:S(2)}, u32[]{:S(2)}) collective-permute-start(bf16[128,768]{1,0:T(8,128)(2,1)S(1)} %get-tuple-element.124), channel_id=1, source_target_pairs={{64,96},{65,97},{66,98},{67,99},{68,100},{69,101},{70,102},{71,103... | collective-permute-start | bytes 589832 | tf_op jit(solution)/shard_map/ppermute | solution.py:45
  97.8 61.8 %collective-permute-start.16 = (bf16[144,768]{1,0:T(8,128)(2,1)S(1)}, bf16[144,768]{1,0:T(8,128)(2,1)S(1)}, u32[]{:S(2)}, u32[]{:S(2)}) collective-permute-start(bf16[144,768]{1,0:T(8,128)(2,1)S(1)} %get-tuple-element.130), channel_id=1, source_target_pairs={{96,131},{97,130},{98,129},{99,128},{100,135},{101,134},{102,133},... | collective-permute-start | bytes 663560 | tf_op jit(solution)/shard_map/ppermute | solution.py:45
  120.7 38.9 %collective-permute-start.13 = (bf16[128,768]{1,0:T(8,128)(2,1)S(1)}, bf16[128,768]{1,0:T(8,128)(2,1)S(1)}, u32[]{:S(2)}, u32[]{:S(2)}) collective-permute-start(bf16[128,768]{1,0:T(8,128)(2,1)S(1)} %get-tuple-element.127), channel_id=1, source_target_pairs={{96,131},{97,130},{98,129},{99,128},{100,135},{101,134},{102,133},... | collective-permute-start | bytes 589832 | tf_op jit(solution)/shard_map/ppermute | solution.py:45
  133.2 90.4 %collective-permute-start.21 = (bf16[144,768]{1,0:T(8,128)(2,1)S(1)}, bf16[144,768]{1,0:T(8,128)(2,1)S(1)}, u32[]{:S(2)}, u32[]{:S(2)}) collective-permute-start(bf16[144,768]{1,0:T(8,128)(2,1)S(1)} %get-tuple-element.135), channel_id=1, source_target_pairs={{64,163},{65,162},{66,161},{67,160},{68,167},{69,166},{70,165},{71... | collective-permute-start | bytes 663560 | tf_op jit(solution)/shard_map/ppermute | solution.py:45
  145.7 78.6 %collective-permute-start.20 = (bf16[144,768]{1,0:T(8,128)(2,1)S(1)}, bf16[144,768]{1,0:T(8,128)(2,1)S(1)}, u32[]{:S(2)}, u32[]{:S(2)}) collective-permute-start(bf16[144,768]{1,0:T(8,128)(2,1)S(1)} %get-tuple-element.134), channel_id=1, source_target_pairs={{96,163},{97,162},{98,161},{99,160},{100,167},{101,166},{102,165},... | collective-permute-start | bytes 663560 | tf_op jit(solution)/shard_map/ppermute | solution.py:45
  162.5 62.5 %collective-permute-start.17 = (bf16[128,768]{1,0:T(8,128)(2,1)S(1)}, bf16[128,768]{1,0:T(8,128)(2,1)S(1)}, u32[]{:S(2)}, u32[]{:S(2)}) collective-permute-start(bf16[128,768]{1,0:T(8,128)(2,1)S(1)} %get-tuple-element.131), channel_id=1, source_target_pairs={{131,163},{130,162},{129,161},{128,160},{135,167},{134,166},{133,1... | collective-permute-start | bytes 589832 | tf_op jit(solution)/shard_map/ppermute | solution.py:45
  198.7 54.0 %collective-permute-start.26 = (bf16[144,768]{1,0:T(8,128)(2,1)S(1)}, bf16[144,768]{1,0:T(8,128)(2,1)S(1)}, u32[]{:S(2)}, u32[]{:S(2)}) collective-permute-start(bf16[144,768]{1,0:T(8,128)(2,1)S(1)} %get-tuple-element.140), channel_id=1, source_target_pairs={{32,195},{33,194},{34,193},{35,192},{36,199},{37,198},{38,197},{39... | collective-permute-start | bytes 663560 | tf_op jit(solution)/shard_map/ppermute | solution.py:45
  211.2 57.9 %collective-permute-start.25 = (bf16[144,768]{1,0:T(8,128)(2,1)S(1)}, bf16[144,768]{1,0:T(8,128)(2,1)S(1)}, u32[]{:S(2)}, u32[]{:S(2)}) collective-permute-start(bf16[144,768]{1,0:T(8,128)(2,1)S(1)} %get-tuple-element.139), channel_id=1, source_target_pairs={{64,195},{65,194},{66,193},{67,192},{68,199},{69,198},{70,197},{71... | collective-permute-start | bytes 663560 | tf_op jit(solution)/shard_map/ppermute | solution.py:45
  227.1 53.9 %collective-permute-start.22 = (bf16[128,768]{1,0:T(8,128)(2,1)S(1)}, bf16[128,768]{1,0:T(8,128)(2,1)S(1)}, u32[]{:S(2)}, u32[]{:S(2)}) collective-permute-start(bf16[128,768]{1,0:T(8,128)(2,1)S(1)} %get-tuple-element.136), channel_id=1, source_target_pairs={{163,195},{162,194},{161,193},{160,192},{167,199},{166,198},{165,1... | collective-permute-start | bytes 589832 | tf_op jit(solution)/shard_map/ppermute | solution.py:45
  251.3 29.7 %collective-permute-start.23 = (bf16[8,768]{1,0:T(8,128)(2,1)S(1)}, bf16[8,768]{1,0:T(8,128)(2,1)S(1)}, u32[]{:S(2)}, u32[]{:S(2)}) collective-permute-start(bf16[8,768]{1,0:T(8,128)(2,1)S(1)} %get-tuple-element.137), channel_id=1, source_target_pairs={{163,194},{162,193},{161,192},{160,199},{167,198},{166,197},{165,1... | collective-permute-start | bytes 36872 | tf_op jit(solution)/shard_map/ppermute | solution.py:45
  252.0 29.1 %collective-permute-start.24 = (bf16[8,768]{1,0:T(8,128)(2,1)S(1)}, bf16[8,768]{1,0:T(8,128)(2,1)S(1)}, u32[]{:S(2)}, u32[]{:S(2)}) collective-permute-start(bf16[8,768]{1,0:T(8,128)(2,1)S(1)} %get-tuple-element.138), channel_id=1, source_target_pairs={{162,195},{161,194},{160,193},{167,192},{166,199},{165,198},{164,1... | collective-permute-start | bytes 36872 | tf_op jit(solution)/shard_map/ppermute | solution.py:45
  252.7 66.6 %collective-permute-start.31 = (bf16[144,768]{1,0:T(8,128)(2,1)}, bf16[144,768]{1,0:T(8,128)(2,1)S(1)}, u32[]{:S(2)}, u32[]{:S(2)}) collective-permute-start(bf16[144,768]{1,0:T(8,128)(2,1)} %get-tuple-element.145), channel_id=1, source_target_pairs={{0,227},{1,226},{2,225},{3,224},{4,231},{5,230},{6,229},{7,228},{8... | collective-permute-start | bytes 663560 | tf_op jit(solution)/shard_map/ppermute | solution.py:45
  269.1 51.5 %collective-permute-start.30 = (bf16[144,768]{1,0:T(8,128)(2,1)}, bf16[144,768]{1,0:T(8,128)(2,1)S(1)}, u32[]{:S(2)}, u32[]{:S(2)}) collective-permute-start(bf16[144,768]{1,0:T(8,128)(2,1)} %get-tuple-element.144), channel_id=1, source_target_pairs={{32,227},{33,226},{34,225},{35,224},{36,231},{37,230},{38,229},{39... | collective-permute-start | bytes 663560 | tf_op jit(solution)/shard_map/ppermute | solution.py:45
  285.5 38.2 %collective-permute-start.27 = (bf16[128,768]{1,0:T(8,128)(2,1)}, bf16[128,768]{1,0:T(8,128)(2,1)}, u32[]{:S(2)}, u32[]{:S(2)}) collective-permute-start(bf16[128,768]{1,0:T(8,128)(2,1)} %get-tuple-element.141), channel_id=1, source_target_pairs={{195,227},{194,226},{193,225},{192,224},{199,231},{198,230},{197,2... | collective-permute-start | bytes 589832 | tf_op jit(solution)/shard_map/ppermute | solution.py:45
  303.5 26.9 %collective-permute-start.36 = (bf16[128,768]{1,0:T(8,128)(2,1)}, bf16[128,768]{1,0:T(8,128)(2,1)}, u32[]{:S(2)}, u32[]{:S(2)}) collective-permute-start(bf16[128,768]{1,0:T(8,128)(2,1)} %dynamic-slice_bitcast_fusion.4), channel_id=1, source_target_pairs={{224,227},{225,226},{226,225},{227,224},{228,231},{229,230},{230,2... | collective-permute-start | bytes 589832 | tf_op jit(solution)/shard_map/ppermute | solution.py:367
  332.1 34.0 %collective-permute-start.39 = (bf16[128,768]{1,0:T(8,128)(2,1)}, bf16[128,768]{1,0:T(8,128)(2,1)}, u32[]{:S(2)}, u32[]{:S(2)}) collective-permute-start(bf16[128,768]{1,0:T(8,128)(2,1)} %get-tuple-element.166), channel_id=1, source_target_pairs={{227,195},{226,194},{225,193},{224,192},{231,199},{230,198},{229,1... | collective-permute-start | bytes 589832 | tf_op jit(solution)/shard_map/ppermute | solution.py:45
  362.8 35.2 %collective-permute-start.32 = (bf16[144,768]{1,0:T(8,128)(2,1)}, bf16[144,768]{1,0:T(8,128)(2,1)}, u32[]{:S(2)}, u32[]{:S(2)}) collective-permute-start(bf16[144,768]{1,0:T(8,128)(2,1)} %select_select_fusion), channel_id=1, source_target_pairs={{0,16},{16,0},{32,48},{48,32},{64,80},{80,64},{96,112},{112,96},{1... | collective-permute-start | bytes 663560 | tf_op jit(solution)/shard_map/ppermute | solution.py:49
  373.9 25.3 %collective-permute-start.42 = (bf16[128,768]{1,0:T(8,128)(2,1)S(1)}, bf16[128,768]{1,0:T(8,128)(2,1)S(1)}, u32[]{:S(2)}, u32[]{:S(2)}) collective-permute-start(bf16[128,768]{1,0:T(8,128)(2,1)S(1)} %get-tuple-element.173), channel_id=1, source_target_pairs={{195,163},{194,162},{193,161},{192,160},{199,167},{198,166},{197,1... | collective-permute-start | bytes 589832 | tf_op jit(solution)/shard_map/ppermute | solution.py:45
  404.9 32.8 %collective-permute-start.45 = (bf16[128,768]{1,0:T(8,128)(2,1)S(1)}, bf16[128,768]{1,0:T(8,128)(2,1)S(1)}, u32[]{:S(2)}, u32[]{:S(2)}) collective-permute-start(bf16[128,768]{1,0:T(8,128)(2,1)S(1)} %get-tuple-element.180), channel_id=1, source_target_pairs={{163,131},{162,130},{161,129},{160,128},{167,135},{166,134},{165,1... | collective-permute-start | bytes 589832 | tf_op jit(solution)/shard_map/ppermute | solution.py:45
  432.1 46.6 %collective-permute-start.33 = (bf16[2,144,192]{2,1,0:T(8,128)(2,1)}, bf16[2,144,192]{2,1,0:T(8,128)(2,1)S(1)}, u32[]{:S(2)}, u32[]{:S(2)}) collective-permute-start(bf16[2,144,192]{2,1,0:T(8,128)(2,1)} %get-tuple-element.246), channel_id=1, source_target_pairs={{0,4},{1,5},{2,6},{3,7},{4,8},{5,9},{6,10},{7,11},{8,12},{9,13},{1... | collective-permute-start | bytes 331784 | tf_op jit(solution)/shard_map/ppermute | solution.py:56
  433.4 45.9 %collective-permute-start.34 = (bf16[2,144,192]{2,1,0:T(8,128)(2,1)}, bf16[2,144,192]{2,1,0:T(8,128)(2,1)}, u32[]{:S(2)}, u32[]{:S(2)}) collective-permute-start(bf16[2,144,192]{2,1,0:T(8,128)(2,1)} %get-tuple-element.245), channel_id=1, source_target_pairs={{0,8},{1,9},{2,10},{3,11},{4,12},{5,13},{6,14},{7,15},{8,0},{9,1},... | collective-permute-start | bytes 331784 | tf_op jit(solution)/shard_map/ppermute | solution.py:56
  435.8 44.2 %collective-permute-start.35 = (bf16[2,144,192]{2,1,0:T(8,128)(2,1)S(1)}, bf16[2,144,192]{2,1,0:T(8,128)(2,1)}, u32[]{:S(2)}, u32[]{:S(2)}) collective-permute-start(bf16[2,144,192]{2,1,0:T(8,128)(2,1)S(1)} %get-tuple-element.244), channel_id=1, source_target_pairs={{0,12},{1,13},{2,14},{3,15},{4,0},{5,1},{6,2},{7,3},{8,4},{9,5},{1... | collective-permute-start | bytes 331784 | tf_op jit(solution)/shard_map/ppermute | solution.py:56
  440.5 68.8 %collective-permute-start.51 = (bf16[144,768]{1,0:T(8,128)(2,1)}, bf16[144,768]{1,0:T(8,128)(2,1)S(1)}, u32[]{:S(2)}, u32[]{:S(2)}) collective-permute-start(bf16[144,768]{1,0:T(8,128)(2,1)} %get-tuple-element.190), channel_id=1, source_target_pairs={{131,96},{130,97},{129,98},{128,99},{135,100},{134,101},{133,102},... | collective-permute-start | bytes 663560 | tf_op jit(solution)/shard_map/ppermute | solution.py:45
  466.1 42.6 %collective-permute-start.48 = (bf16[128,768]{1,0:T(8,128)(2,1)}, bf16[128,768]{1,0:T(8,128)(2,1)S(1)}, u32[]{:S(2)}, u32[]{:S(2)}) collective-permute-start(bf16[128,768]{1,0:T(8,128)(2,1)} %get-tuple-element.187), channel_id=1, source_target_pairs={{131,96},{130,97},{129,98},{128,99},{135,100},{134,101},{133,102},... | collective-permute-start | bytes 589832 | tf_op jit(solution)/shard_map/ppermute | solution.py:45
  478.6 16.8 %collective-permute-start.49 = (bf16[8,768]{1,0:T(8,128)(2,1)S(1)}, bf16[8,768]{1,0:T(8,128)(2,1)S(1)}, u32[]{:S(2)}, u32[]{:S(2)}) collective-permute-start(bf16[8,768]{1,0:T(8,128)(2,1)S(1)} %get-tuple-element.188), channel_id=1, source_target_pairs={{131,97},{130,98},{129,99},{128,100},{135,101},{134,102},{133,103}... | collective-permute-start | bytes 36872 | tf_op jit(solution)/shard_map/ppermute | solution.py:45
  479.3 29.3 %collective-permute-start.50 = (bf16[8,768]{1,0:T(8,128)(2,1)S(1)}, bf16[8,768]{1,0:T(8,128)(2,1)S(1)}, u32[]{:S(2)}, u32[]{:S(2)}) collective-permute-start(bf16[8,768]{1,0:T(8,128)(2,1)S(1)} %get-tuple-element.189), channel_id=1, source_target_pairs={{130,96},{129,97},{128,98},{135,99},{134,100},{133,101},{132,102},... | collective-permute-start | bytes 36872 | tf_op jit(solution)/shard_map/ppermute | solution.py:45
  481.1 63.4 %collective-permute-start.56 = (bf16[144,768]{1,0:T(8,128)(2,1)}, bf16[144,768]{1,0:T(8,128)(2,1)S(1)}, u32[]{:S(2)}, u32[]{:S(2)}) collective-permute-start(bf16[144,768]{1,0:T(8,128)(2,1)} %copy-done.55), channel_id=1, source_target_pairs={{163,64},{162,65},{161,66},{160,67},{167,68},{166,69},{165,70},{16... | collective-permute-start | bytes 663560 | tf_op jit(solution)/shard_map/ppermute | solution.py:45
  495.5 62.2 %collective-permute-start.55 = (bf16[144,768]{1,0:T(8,128)(2,1)}, bf16[144,768]{1,0:T(8,128)(2,1)}, u32[]{:S(2)}, u32[]{:S(2)}) collective-permute-start(bf16[144,768]{1,0:T(8,128)(2,1)} %copy-done.56), channel_id=1, source_target_pairs={{131,64},{130,65},{129,66},{128,67},{135,68},{134,69},{133,70},{13... | collective-permute-start | bytes 663560 | tf_op jit(solution)/shard_map/ppermute | solution.py:45
  516.6 54.9 %collective-permute-start.52 = (bf16[128,768]{1,0:T(8,128)(2,1)}, bf16[128,768]{1,0:T(8,128)(2,1)S(1)}, u32[]{:S(2)}, u32[]{:S(2)}) collective-permute-start(bf16[128,768]{1,0:T(8,128)(2,1)} %get-tuple-element.195), channel_id=1, source_target_pairs={{96,64},{97,65},{98,66},{99,67},{100,68},{101,69},{102,70},{103,71... | collective-permute-start | bytes 589832 | tf_op jit(solution)/shard_map/ppermute | solution.py:45
  533.4 38.1 %collective-permute-start.53 = (bf16[8,768]{1,0:T(8,128)(2,1)S(1)}, bf16[8,768]{1,0:T(8,128)(2,1)S(1)}, u32[]{:S(2)}, u32[]{:S(2)}) collective-permute-start(bf16[8,768]{1,0:T(8,128)(2,1)S(1)} %get-tuple-element.196), channel_id=1, source_target_pairs={{96,65},{97,66},{98,67},{99,68},{100,69},{101,70},{102,71},{103,72... | collective-permute-start | bytes 36872 | tf_op jit(solution)/shard_map/ppermute | solution.py:45
  534.0 37.5 %collective-permute-start.54 = (bf16[8,768]{1,0:T(8,128)(2,1)S(1)}, bf16[8,768]{1,0:T(8,128)(2,1)S(1)}, u32[]{:S(2)}, u32[]{:S(2)}) collective-permute-start(bf16[8,768]{1,0:T(8,128)(2,1)S(1)} %get-tuple-element.197), channel_id=1, source_target_pairs={{97,64},{98,65},{99,66},{100,67},{101,68},{102,69},{103,70},{104,7... | collective-permute-start | bytes 36872 | tf_op jit(solution)/shard_map/ppermute | solution.py:45
  544.5 63.1 %collective-permute-start.61 = (bf16[144,768]{1,0:T(8,128)(2,1)}, bf16[144,768]{1,0:T(8,128)(2,1)}, u32[]{:S(2)}, u32[]{:S(2)}) collective-permute-start(bf16[144,768]{1,0:T(8,128)(2,1)} %copy-done.53), channel_id=1, source_target_pairs={{195,32},{194,33},{193,34},{192,35},{199,36},{198,37},{197,38},{19... | collective-permute-start | bytes 663560 | tf_op jit(solution)/shard_map/ppermute | solution.py:45
  557.7 62.4 %collective-permute-start.60 = (bf16[144,768]{1,0:T(8,128)(2,1)}, bf16[144,768]{1,0:T(8,128)(2,1)}, u32[]{:S(2)}, u32[]{:S(2)}) collective-permute-start(bf16[144,768]{1,0:T(8,128)(2,1)} %copy-done.54), channel_id=1, source_target_pairs={{163,32},{162,33},{161,34},{160,35},{167,36},{166,37},{165,38},{16... | collective-permute-start | bytes 663560 | tf_op jit(solution)/shard_map/ppermute | solution.py:45
  579.5 53.5 %collective-permute-start.57 = (bf16[128,768]{1,0:T(8,128)(2,1)}, bf16[128,768]{1,0:T(8,128)(2,1)S(1)}, u32[]{:S(2)}, u32[]{:S(2)}) collective-permute-start(bf16[128,768]{1,0:T(8,128)(2,1)} %get-tuple-element.204), channel_id=1, source_target_pairs={{64,32},{65,33},{66,34},{67,35},{68,36},{69,37},{70,38},{71,39},{7... | collective-permute-start | bytes 589832 | tf_op jit(solution)/shard_map/ppermute | solution.py:45
  597.3 35.7 %collective-permute-start.58 = (bf16[8,768]{1,0:T(8,128)(2,1)}, bf16[8,768]{1,0:T(8,128)(2,1)S(1)}, u32[]{:S(2)}, u32[]{:S(2)}) collective-permute-start(bf16[8,768]{1,0:T(8,128)(2,1)} %get-tuple-element.205), channel_id=1, source_target_pairs={{64,33},{65,34},{66,35},{67,36},{68,37},{69,38},{70,39},{71,40},{7... | collective-permute-start | bytes 36872 | tf_op jit(solution)/shard_map/ppermute | solution.py:45
  598.0 35.0 %collective-permute-start.59 = (bf16[8,768]{1,0:T(8,128)(2,1)}, bf16[8,768]{1,0:T(8,128)(2,1)S(1)}, u32[]{:S(2)}, u32[]{:S(2)}) collective-permute-start(bf16[8,768]{1,0:T(8,128)(2,1)} %get-tuple-element.206), channel_id=1, source_target_pairs={{65,32},{66,33},{67,34},{68,35},{69,36},{70,37},{71,38},{72,39},{7... | collective-permute-start | bytes 36872 | tf_op jit(solution)/shard_map/ppermute | solution.py:45
  607.6 58.1 %collective-permute-start.66 = (bf16[144,768]{1,0:T(8,128)(2,1)}, bf16[144,768]{1,0:T(8,128)(2,1)S(1)}, u32[]{:S(2)}, u32[]{:S(2)}) collective-permute-start(bf16[144,768]{1,0:T(8,128)(2,1)} %copy-done.51), channel_id=1, source_target_pairs={{227,0},{226,1},{225,2},{224,3},{231,4},{230,5},{229,6},{228,7},{2... | collective-permute-start | bytes 663560 | tf_op jit(solution)/shard_map/ppermute | solution.py:45
  620.1 45.7 %collective-permute-start.65 = (bf16[144,768]{1,0:T(8,128)(2,1)}, bf16[144,768]{1,0:T(8,128)(2,1)}, u32[]{:S(2)}, u32[]{:S(2)}) collective-permute-start(bf16[144,768]{1,0:T(8,128)(2,1)} %copy-done.52), channel_id=1, source_target_pairs={{195,0},{194,1},{193,2},{192,3},{199,4},{198,5},{197,6},{196,7},{2... | collective-permute-start | bytes 663560 | tf_op jit(solution)/shard_map/ppermute | solution.py:45
  642.0 25.1 %collective-permute-start.62 = (bf16[128,768]{1,0:T(8,128)(2,1)}, bf16[128,768]{1,0:T(8,128)(2,1)}, u32[]{:S(2)}, u32[]{:S(2)}) collective-permute-start(bf16[128,768]{1,0:T(8,128)(2,1)} %get-tuple-element.213), channel_id=1, source_target_pairs={{32,0},{33,1},{34,2},{35,3},{36,4},{37,5},{38,6},{39,7},{40,8},{41... | collective-permute-start | bytes 589832 | tf_op jit(solution)/shard_map/ppermute | solution.py:45
  685.8 20.5 %collective-permute-start.69 = (bf16[264,768]{1,0:T(8,128)(2,1)S(1)}, bf16[264,768]{1,0:T(8,128)(2,1)S(1)}, u32[]{:S(2)}, u32[]{:S(2)}) collective-permute-start(bf16[264,768]{1,0:T(8,128)(2,1)S(1)} %pad_maximum_fusion.2.refs_0_), channel_id=1, source_target_pairs={{0,8},{1,9},{2,10},{3,11},{4,12},{5,13},{6,14},{7,15},{8,0},{9,1},... | collective-permute-start | bytes 1216520 | tf_op jit(solution)/shard_map/ppermute | solution.py:56
  688.6 17.8 %collective-permute-start.70 = (bf16[264,768]{1,0:T(8,128)(2,1)S(1)}, bf16[264,768]{1,0:T(8,128)(2,1)S(1)}, u32[]{:S(2)}, u32[]{:S(2)}) collective-permute-start(bf16[264,768]{1,0:T(8,128)(2,1)S(1)} %pad_maximum_fusion.2.refs_0_), channel_id=1, source_target_pairs={{0,12},{1,13},{2,14},{3,15},{4,0},{5,1},{6,2},{7,3},{8,4},{9,5},{1... | collective-permute-start | bytes 1216520 | tf_op jit(solution)/shard_map/ppermute | solution.py:56
  708.1 32.0 %collective-permute-start.71 = (bf16[248,768]{1,0:T(8,128)(2,1)S(1)}, bf16[248,768]{1,0:T(8,128)(2,1)S(1)}, u32[]{:S(2)}, u32[]{:S(2)}) collective-permute-start(bf16[248,768]{1,0:T(8,128)(2,1)S(1)} %get-tuple-element.231), channel_id=1, source_target_pairs={{0,1},{1,2},{2,3},{3,0},{4,5},{5,6},{6,7},{7,4},{8,9},{9,10},{10,1... | collective-permute-start | bytes 1142792 | tf_op jit(solution)/shard_map/ppermute | solution.py:63
  716.4 31.6 %collective-permute-start.72 = (bf16[248,768]{1,0:T(8,128)(2,1)S(1)}, bf16[248,768]{1,0:T(8,128)(2,1)S(1)}, u32[]{:S(2)}, u32[]{:S(2)}) collective-permute-start(bf16[248,768]{1,0:T(8,128)(2,1)S(1)} %get-tuple-element.232), channel_id=1, source_target_pairs={{0,2},{1,3},{2,0},{3,1},{4,6},{5,7},{6,4},{7,5},{8,10},{9,11},{10,... | collective-permute-start | bytes 1142792 | tf_op jit(solution)/shard_map/ppermute | solution.py:63
  728.2 28.4 %collective-permute-start.73 = (bf16[248,768]{1,0:T(8,128)(2,1)S(1)}, bf16[248,768]{1,0:T(8,128)(2,1)S(1)}, u32[]{:S(2)}, u32[]{:S(2)}) collective-permute-start(bf16[248,768]{1,0:T(8,128)(2,1)S(1)} %get-tuple-element.233), channel_id=1, source_target_pairs={{0,3},{1,0},{2,1},{3,2},{4,7},{5,4},{6,5},{7,6},{8,11},{9,8},{10,9... | collective-permute-start | bytes 1142792 | tf_op jit(solution)/shard_map/ppermute | solution.py:63
  (91 other events, 1189.9 us)
